TPU v7x, 512 devices: a whole 4x8x8 slice. The times are simulated.
512 devices in a mesh: pages: 64 (over y, z_lo, core), heads: 8 (over x, z_hi).
Axes of the slice: x: 4, y: 8, z: 8 (z_hi: 2, z_lo: 4; z = z_hi * 4 + z_lo), core: 2. Of those that a mesh axis runs over, the one named last changes fastest.
Arguments:
- candidates: bfloat16 [49152, 1024], P(('pages', 'heads')), may hold values from -6 to 6
- in_weight: bfloat16 [2, 1024, 8, 512], P(None, None, 'heads'), may hold values from -0.1875 to 0.1875
- out_weight: bfloat16 [2, 8, 128, 1024], P(None, 'heads'), may hold values from -0.1875 to 0.1875
- page_cache: bfloat16 [2, 4096, 8, 2, 32, 128], P(None, 'pages', 'heads'), may hold values from -6 to 6
- page_lists: int32 [1024, 4], P('pages'), may hold values from 0 to 4095, as said below
- hist_len: int32 [1024], P('pages'), may hold values from 1 to 128
Outputs:
- hidden_out: bfloat16 [49152, 1024], P(('pages', 'heads'))
Inputs may be any that keep to these rules, and one draw needn't show every extreme that they name: `page_lists`: every page id appears in exactly one list. Page p lies on index p // 64 of pages; the requests of one index of pages list either none or exactly 2 pages that lie on any one index.
All inputs are finite; a program needn't handle non-finite values.
Results may differ from a plain program's by a relative error of at most 0.018.
Values may be sent and summed in bfloat16 or wider, within the bound.
A program may use at most 64 MiB of HBM per device.

v0:
```python
import math

import jax
import jax.numpy as jnp
from jax import lax
from jax.sharding import PartitionSpec as P

eps = 1e-05


def layer_norm(values):
    row_mean = jnp.mean(values, -1, keepdims=True)
    centred = values - row_mean
    spread = jnp.mean(centred * centred, -1, keepdims=True)
    return centred * lax.rsqrt(spread + eps)


def on_device(candidates, in_weight, out_weight, page_cache, page_lists, hist_len):
    readers = lax.axis_size("pages")
    head_group = lax.axis_size("heads")
    layers = in_weight.shape[0]
    model_width = in_weight.shape[1]
    heads_here = in_weight.shape[2]
    head_dim = out_weight.shape[2]
    pages_here = page_cache.shape[1]
    page_len = page_cache.shape[4]
    requests, max_pages = page_lists.shape
    slot_count = requests * max_pages
    capacity = 2 * slot_count // readers
    shard_rows = candidates.shape[0]
    cand_rows = shard_rows * head_group
    per_request = cand_rows // requests
    score_scale = 1.0 / math.sqrt(head_dim)
    flat_ids = page_lists.reshape(slot_count)
    slot_owner = flat_ids // pages_here
    local_ids = flat_ids % pages_here
    slot_order = jnp.arange(slot_count)
    earlier_same = (slot_owner[None, :] == slot_owner[:, None]) & (
        slot_order[None, :] < slot_order[:, None]
    )
    slot_rank = jnp.sum(earlier_same.astype(jnp.int32), axis=1)
    places = slot_owner * capacity + slot_rank
    divisors = (hist_len + 1).astype(jnp.float32)
    cand_divisors = jnp.repeat(divisors, per_request)
    slot_targets = jnp.arange(readers * capacity)
    matches = places[None, :] == slot_targets[:, None]
    filled = jnp.any(matches, axis=1)
    inverse = jnp.sum(jnp.where(matches, slot_order[None, :], 0), axis=1)
    asked_request = inverse // max_pages
    page_of_slot = slot_order % max_pages
    valid_tokens = jnp.clip(jnp.repeat(hist_len, max_pages) - page_of_slot * page_len, 0, page_len)
    slot_meta = jnp.stack(
        [
            jnp.take(local_ids, inverse),
            jnp.take(valid_tokens, inverse),
            jnp.take(hist_len, asked_request),
        ],
        axis=-1,
    )
    slot_meta = jnp.where(filled[:, None], slot_meta, 0).reshape(readers, capacity, 3)
    hidden_rows = candidates
    for layer_index in range(layers):
        weights_in = in_weight[layer_index].reshape(model_width, heads_here * 4 * head_dim)
        ready = layer_norm(
            lax.all_gather(hidden_rows, "heads", axis=0, tiled=True).astype(jnp.float32)
        ).astype(jnp.bfloat16)
        projected = jax.nn.silu(jnp.dot(ready, weights_in, preferred_element_type=jnp.float32))
        projected = projected.reshape(cand_rows, heads_here, 4 * head_dim)
        gate_part = projected[:, :, :head_dim]
        value_part = projected[:, :, head_dim : 2 * head_dim].astype(jnp.bfloat16)
        query_part = projected[:, :, 2 * head_dim : 3 * head_dim].astype(jnp.bfloat16)
        key_part = projected[:, :, 3 * head_dim :].astype(jnp.bfloat16)
        queries = query_part.reshape(requests, per_request, heads_here, head_dim)
        sent_queries = jnp.take(queries, asked_request, axis=0)
        sent_queries = jnp.where(
            filled[:, None, None, None], sent_queries, jnp.zeros((), jnp.bfloat16)
        )
        sent_queries = sent_queries.reshape(readers, capacity, per_request, heads_here, head_dim)
        got_queries, got_meta = (
            lax.all_to_all(sent_queries, "pages", split_axis=0, concat_axis=0, tiled=True),
            lax.all_to_all(slot_meta, "pages", split_axis=0, concat_axis=0, tiled=True),
        )
        page_rows = jnp.take(
            page_cache[layer_index], got_meta[:, :, 0].reshape(readers * capacity), axis=0
        )
        page_rows = page_rows.reshape(readers, capacity, heads_here, 2, page_len, head_dim)
        scores = (
            jnp.einsum(
                "ncqhd,nchtd->nchqt",
                got_queries,
                page_rows[:, :, :, 0],
                preferred_element_type=jnp.float32,
            )
            * score_scale
        )
        keep_mask = jnp.arange(page_len)[None, None, :] < got_meta[:, :, 1][:, :, None]
        owner_divisors = (got_meta[:, :, 2] + 1).astype(jnp.float32)
        weights = (
            jnp.where(keep_mask[:, :, None, None, :], jax.nn.silu(scores), 0.0)
            / owner_divisors[:, :, None, None, None]
        )
        weights = weights.astype(jnp.bfloat16)
        partial_out = jnp.einsum(
            "nchqt,nchtd->ncqhd", weights, page_rows[:, :, :, 1], preferred_element_type=jnp.float32
        )
        returned = lax.all_to_all(
            partial_out.astype(jnp.bfloat16), "pages", split_axis=0, concat_axis=0, tiled=True
        ).astype(partial_out.dtype)
        returned_rows = jnp.take(
            returned.reshape(readers * capacity, per_request, heads_here, head_dim), places, axis=0
        )
        attended_hist = jnp.sum(
            returned_rows.reshape(requests, max_pages, per_request, heads_here, head_dim), axis=1
        )
        attended = attended_hist.reshape(cand_rows, heads_here, head_dim)
        self_score = (
            jnp.sum(query_part.astype(jnp.float32) * key_part.astype(jnp.float32), -1) * score_scale
        )
        self_weight = (jax.nn.silu(self_score) / cand_divisors[:, None]).astype(jnp.bfloat16)
        attended = attended + self_weight.astype(jnp.float32)[:, :, None] * value_part.astype(
            jnp.float32
        )
        gated_rows = (
            (layer_norm(attended) * gate_part)
            .astype(jnp.bfloat16)
            .reshape(cand_rows, heads_here * head_dim)
        )
        weights_out = out_weight[layer_index].reshape(heads_here * head_dim, model_width)
        summed = lax.psum_scatter(
            jnp.dot(gated_rows, weights_out, preferred_element_type=jnp.float32).astype(
                jnp.bfloat16
            ),
            "heads",
            scatter_dimension=0,
            tiled=True,
        ).astype(jnp.float32)
        hidden_rows = (hidden_rows.astype(jnp.float32) + summed).astype(jnp.bfloat16)
    return hidden_rows


def solution(mesh):
    in_specs = (
        P(("pages", "heads"), None),
        P(None, None, "heads", None),
        P(None, "heads", None, None),
        P(None, "pages", "heads", None, None, None),
        P("pages", None),
        P("pages"),
    )
    out_specs = P(("pages", "heads"), None)
    return jax.shard_map(
        on_device, mesh=mesh, in_specs=in_specs, out_specs=out_specs, check_vma=False
    )
```

profile of v0, /device:TPU:6, one launch (start us, length us, event | category | flops | bytes accessed | tf_op | source)
XLA Modules:
  0.0 597.2 jit_solution(8234759997289166943)
XLA Ops:
  11.9 2.0 fusion.69
  13.8 10.1 %broadcast_select_fusion.1 = (s32[128]{0:T(128)S(1)}, s32[128]{0:T(128)S(1)}, s32[128]{0:T(128)S(1)}) fusion(s32[128]{0:T(128)S(1)} %gather_fusion, s32[128]{0:T(128)S(1)} %select_reduce_fusion, s32[128]{0:T(128)S(1)} %gather_fusion.1, s32[]{:T(128)} %bitcast.25, s32[]{:T(128)} %bitcast.24, s32[]{:T(128)} %bitcast.23, s32[]{:T(128)} %bitcast.22, ...), kind=kLoop, calls=%fused_computation.158 | loop fusion | flops 7168 | bytes 3136 | tf_op jit(solution)/shard_map/jit(_take)/select_n | solution.py:54
  25.8 13.5 %all-to-all-start = ((s32[64,2,3]{2,1,0:T(2,128)}), s32[64,2,3]{2,1,0:T(2,128)S(1)}, u32[]{:S(2)}, u32[]{:S(2)}) async-start(s32[64,2,3]{2,1,0:T(2,128)} %copy.62), calls=%async_computation | async-start | bytes 131072 | tf_op jit(solution)/shard_map/all_to_all | solution.py:81
  39.4 50.4 %all-gather.3.cloned.1.call-done = bf16[768,1024]{1,0:T(8,128)(2,1)} async-done(((bf16[96,1024]{1,0:T(8,128)(2,1)}), bf16[768,1024]{1,0:T(8,128)(2,1)}) %all-gather.3.cloned.1.call-update) | async-done | bytes 1572880 | tf_op jit(solution)/shard_map/all_gather | solution.py:65
  92.2 3.6 fusion.70
  98.4 8.5 %all-to-all-start.1 = ((bf16[64,2,48,1,128]{4,2,1,3,0:T(8,128)(2,1)}), bf16[64,2,48,1,128]{4,2,1,3,0:T(8,128)(2,1)}, u32[]{:S(2)}, u32[]{:S(2)}) async-start(bf16[64,2,48,1,128]{4,2,1,3,0:T(8,128)(2,1)} %bitcast.38), calls=%async_computation.1 | async-start | bytes 3145728 | tf_op jit(solution)/shard_map/all_to_all | solution.py:80
  106.9 2.0 slice_bitcast_fusion.8
  110.3 2.1 gather_fusion.2
  112.5 2.2 gather_fusion.5
  114.6 2.7 bitcast_select_fusion
  119.5 26.5 %all-to-all-done.1 = bf16[64,2,48,1,128]{4,2,1,3,0:T(8,128)(2,1)} async-done(((bf16[64,2,48,1,128]{4,2,1,3,0:T(8,128)(2,1)}), bf16[64,2,48,1,128]{4,2,1,3,0:T(8,128)(2,1)}, u32[]{:S(2)}, u32[]{:S(2)}) %all-to-all-start.1) | async-done | bytes 1572896 | tf_op jit(solution)/shard_map/all_to_all | solution.py:80
  146.0 4.0 fusion.20
  150.0 6.9 %all-to-all-start.2 = ((bf16[64,2,48,1,128]{4,2,1,3,0:T(8,128)(2,1)}), bf16[64,2,48,1,128]{4,2,1,3,0:T(8,128)(2,1)}, u32[]{:S(2)}, u32[]{:S(2)}) async-start(bf16[64,2,48,1,128]{4,2,1,3,0:T(8,128)(2,1)} %fusion.20), calls=%async_computation.2 | async-start | bytes 3145728 | tf_op jit(solution)/shard_map/all_to_all | solution.py:106
  157.5 38.5 %all-to-all-done.2 = bf16[64,2,48,1,128]{4,2,1,3,0:T(8,128)(2,1)} async-done(((bf16[64,2,48,1,128]{4,2,1,3,0:T(8,128)(2,1)}), bf16[64,2,48,1,128]{4,2,1,3,0:T(8,128)(2,1)}, u32[]{:S(2)}, u32[]{:S(2)}) %all-to-all-start.2) | async-done | bytes 1572896 | tf_op jit(solution)/shard_map/all_to_all | solution.py:106
  196.0 3.3 bitcast_convert_fusion.1
  199.3 3.7 gather_fusion.4
  203.0 2.8 bitcast_select_fusion.4
  208.4 2.8 convolution_convert_fusion.3
  211.3 92.4 %reduce-scatter.3.cloned.1.call-done = bf16[96,1024]{1,0:T(8,128)(2,1)} async-done(((bf16[768,1024]{1,0:T(8,128)(2,1)}), bf16[96,1024]{1,0:T(8,128)(2,1)}) %reduce-scatter.3.cloned.1.call-update) | async-done | bytes 196624 | tf_op jit(solution)/shard_map/reduce_scatter | solution.py:129
  305.4 71.9 %all-gather.5.cloned.1.call-done = bf16[768,1024]{1,0:T(8,128)(2,1)} async-done(((bf16[96,1024]{1,0:T(8,128)(2,1)}), bf16[768,1024]{1,0:T(8,128)(2,1)}) %all-gather.5.cloned.1.call-update) | async-done | bytes 1572880 | tf_op jit(solution)/shard_map/all_gather | solution.py:65
  379.8 3.6 fusion.71
  383.4 1.9 gather_fusion.6
  385.3 2.7 fusion.13
  388.1 8.5 %all-to-all-start.3 = ((bf16[64,2,48,1,128]{4,2,1,3,0:T(8,128)(2,1)}), bf16[64,2,48,1,128]{4,2,1,3,0:T(8,128)(2,1)}, u32[]{:S(2)}, u32[]{:S(2)}) async-start(bf16[64,2,48,1,128]{4,2,1,3,0:T(8,128)(2,1)} %bitcast.191), calls=%async_computation.4 | async-start | bytes 3145728 | tf_op jit(solution)/shard_map/all_to_all | solution.py:80
  398.3 37.4 %all-to-all-done.3 = bf16[64,2,48,1,128]{4,2,1,3,0:T(8,128)(2,1)} async-done(((bf16[64,2,48,1,128]{4,2,1,3,0:T(8,128)(2,1)}), bf16[64,2,48,1,128]{4,2,1,3,0:T(8,128)(2,1)}, u32[]{:S(2)}, u32[]{:S(2)}) %all-to-all-start.3) | async-done | bytes 1572896 | tf_op jit(solution)/shard_map/all_to_all | solution.py:80
  435.7 4.0 fusion.21
  439.7 6.5 %all-to-all-start.4 = ((bf16[64,2,48,1,128]{4,2,1,3,0:T(8,128)(2,1)}), bf16[64,2,48,1,128]{4,2,1,3,0:T(8,128)(2,1)S(1)}, u32[]{:S(2)}, u32[]{:S(2)}) async-start(bf16[64,2,48,1,128]{4,2,1,3,0:T(8,128)(2,1)} %fusion.21), calls=%async_computation.5 | async-start | bytes 3145728 | tf_op jit(solution)/shard_map/all_to_all | solution.py:106
  446.4 39.1 %all-to-all-done.4 = bf16[64,2,48,1,128]{4,2,1,3,0:T(8,128)(2,1)S(1)} async-done(((bf16[64,2,48,1,128]{4,2,1,3,0:T(8,128)(2,1)}), bf16[64,2,48,1,128]{4,2,1,3,0:T(8,128)(2,1)S(1)}, u32[]{:S(2)}, u32[]{:S(2)}) %all-to-all-start.4) | async-done | bytes 1572896 | tf_op jit(solution)/shard_map/all_to_all | solution.py:106
  485.5 2.0 bitcast_convert_fusion
  487.5 2.5 gather_fusion.7
  493.6 2.8 convolution_convert_fusion.2
  496.5 92.5 %reduce-scatter.5.cloned.1.call-done = bf16[96,1024]{1,0:T(8,128)(2,1)} async-done(((bf16[768,1024]{1,0:T(8,128)(2,1)}), bf16[96,1024]{1,0:T(8,128)(2,1)}) %reduce-scatter.5.cloned.1.call-update) | async-done | bytes 196624 | tf_op jit(solution)/shard_map/reduce_scatter | solution.py:129
  (99 shorter events, 30.3 us)
Async XLA Ops:
  6.5 83.3 %all-gather.3.cloned.1.call-start = ((), (), s32[]{:S(2)}) async-start(), calls=%async_computation.7 | async-start | bytes 1769472 | tf_op jit(solution)/shard_map/all_gather | solution.py:65
  25.8 72.6 %all-to-all-start = ((s32[64,2,3]{2,1,0:T(2,128)}), s32[64,2,3]{2,1,0:T(2,128)S(1)}, u32[]{:S(2)}, u32[]{:S(2)}) async-start(s32[64,2,3]{2,1,0:T(2,128)} %copy.62), calls=%async_computation | async-start | bytes 131072 | tf_op jit(solution)/shard_map/all_to_all | solution.py:81
  89.8 1.9 copy-start
  98.4 47.6 %all-to-all-start.1 = ((bf16[64,2,48,1,128]{4,2,1,3,0:T(8,128)(2,1)}), bf16[64,2,48,1,128]{4,2,1,3,0:T(8,128)(2,1)}, u32[]{:S(2)}, u32[]{:S(2)}) async-start(bf16[64,2,48,1,128]{4,2,1,3,0:T(8,128)(2,1)} %bitcast.38), calls=%async_computation.1 | async-start | bytes 3145728 | tf_op jit(solution)/shard_map/all_to_all | solution.py:80
  150.0 7.1 %copy-start.6 = (s32[16]{0:T(128)S(1)}, s32[16]{0:T(128)}, u32[]{:S(2)}) copy-start(s32[16]{0:T(128)} %param.19) | copy-start | bytes 196
  150.0 46.0 %all-to-all-start.2 = ((bf16[64,2,48,1,128]{4,2,1,3,0:T(8,128)(2,1)}), bf16[64,2,48,1,128]{4,2,1,3,0:T(8,128)(2,1)}, u32[]{:S(2)}, u32[]{:S(2)}) async-start(bf16[64,2,48,1,128]{4,2,1,3,0:T(8,128)(2,1)} %fusion.20), calls=%async_computation.2 | async-start | bytes 3145728 | tf_op jit(solution)/shard_map/all_to_all | solution.py:106
  156.9 146.8 %reduce-scatter.3.cloned.1.call-start = ((), (), s32[]{:S(2)}) async-start(), calls=%async_computation.8 | async-start | bytes 1769472 | tf_op jit(solution)/shard_map/reduce_scatter | solution.py:129
  207.4 1.0 copy-start.4
  208.4 95.3 %copy-start.3 = (bf16[96,1024]{1,0:T(8,128)(2,1)S(1)}, bf16[96,1024]{1,0:T(8,128)(2,1)}, u32[]{:S(2)}) copy-start(bf16[96,1024]{1,0:T(8,128)(2,1)} %param.14) | copy-start | bytes 589828
  211.2 166.1 %all-gather.5.cloned.1.call-start = ((), (), s32[]{:S(2)}) async-start(), calls=%async_computation.9 | async-start | bytes 1769472 | tf_op jit(solution)/shard_map/all_gather | solution.py:65
  377.3 1.9 copy-start.1
  388.1 47.6 %all-to-all-start.3 = ((bf16[64,2,48,1,128]{4,2,1,3,0:T(8,128)(2,1)}), bf16[64,2,48,1,128]{4,2,1,3,0:T(8,128)(2,1)}, u32[]{:S(2)}, u32[]{:S(2)}) async-start(bf16[64,2,48,1,128]{4,2,1,3,0:T(8,128)(2,1)} %bitcast.191), calls=%async_computation.4 | async-start | bytes 3145728 | tf_op jit(solution)/shard_map/all_to_all | solution.py:80
  439.7 45.8 %all-to-all-start.4 = ((bf16[64,2,48,1,128]{4,2,1,3,0:T(8,128)(2,1)}), bf16[64,2,48,1,128]{4,2,1,3,0:T(8,128)(2,1)S(1)}, u32[]{:S(2)}, u32[]{:S(2)}) async-start(bf16[64,2,48,1,128]{4,2,1,3,0:T(8,128)(2,1)} %fusion.21), calls=%async_computation.5 | async-start | bytes 3145728 | tf_op jit(solution)/shard_map/all_to_all | solution.py:106
  446.2 142.8 %reduce-scatter.5.cloned.1.call-start = ((), (), s32[]{:S(2)}) async-start(), calls=%async_computation.10 | async-start | bytes 1769472 | tf_op jit(solution)/shard_map/reduce_scatter | solution.py:129
  491.4 2.2 copy-start.5
  493.6 95.4 %copy-start.2 = (bf16[96,1024]{1,0:T(8,128)(2,1)S(1)}, bf16[96,1024]{1,0:T(8,128)(2,1)}, u32[]{:S(2)}) copy-start(bf16[96,1024]{1,0:T(8,128)(2,1)} %add_convert_fusion.1) | copy-start | bytes 589828
Sparse Core Ops, SparseCore 0:
  10.5 79.2 all-gather.2
  211.4 92.3 reduce-scatter.2
  306.9 70.3 all-gather.4
  496.6 92.3 reduce-scatter.4
where the time goes:
time: 599 us; the launch traced here: 597 us
  waiting for transfers between devices  449 us (75%)
  starting transfers between devices  44.2 us (7%)
  other arithmetic  39.9 us (7%)
  local copies, waits for them, and re-layouts  29.2 us (5%)
  matrix products  20.9 us (3%)
  between operations  13.5 us (2%)
    reduce_scatter x2, waiting for transfers between devices, on_device(): lax.psum_scatter(jnp.dot(gated_rows, weights_out, preferred_element_type=...  185 us
    all_gather x2, waiting for transfers between devices, on_device(): lax.all_gather(hidden_rows, 'heads', axis=0, tiled=True).astype(jnp.float32)  122 us
    all_to_all x2, waiting for transfers between devices, on_device(): lax.all_to_all(partial_out.astype(jnp.bfloat16), 'pages', split_axis=0, c...  77.6 us
    all_to_all x2, waiting for transfers between devices, on_device(): lax.all_to_all(sent_queries, 'pages', split_axis=0, concat_axis=0, tiled=...  63.9 us
    all_to_all x2, starting transfers between devices, on_device(): lax.all_to_all(sent_queries, 'pages', split_axis=0, concat_axis=0, tiled=...  17 us
    all_to_all x1, starting transfers between devices, on_device(): lax.all_to_all(slot_meta, 'pages', split_axis=0, concat_axis=0, tiled=True)  13.5 us
    all_to_all x2, starting transfers between devices, on_device(): lax.all_to_all(partial_out.astype(jnp.bfloat16), 'pages', split_axis=0, c...  13.3 us
  transfers between devices with their start and end apart: 9, of which 8 were waited for; matrix products, arithmetic and copies ran while one was open for 7% of the time, Pallas kernels for 0%

commit v1 on v0

v1 whole, which is shorter than its diff:
```python
import math

import jax
import jax.numpy as jnp
from jax import lax
from jax.sharding import PartitionSpec as P

eps = 1e-05


def layer_norm(values):
    row_mean = jnp.mean(values, -1, keepdims=True)
    centred = values - row_mean
    spread = jnp.mean(centred * centred, -1, keepdims=True)
    return centred * lax.rsqrt(spread + eps)


def gather_rows(rows):
    return lax.all_gather(rows, "heads", axis=0, tiled=True)


def scatter_sum(terms):
    return lax.psum_scatter(terms, "heads", scatter_dimension=0, tiled=True).astype(jnp.float32)


def on_device(candidates, in_weight, out_weight, page_cache, page_lists, hist_len):
    readers = lax.axis_size("pages")
    head_group = lax.axis_size("heads")
    layers = in_weight.shape[0]
    model_width = in_weight.shape[1]
    head_dim = out_weight.shape[2]
    pages_here = page_cache.shape[1]
    page_len = page_cache.shape[4]
    requests, max_pages = page_lists.shape
    slot_count = requests * max_pages
    capacity = 2 * slot_count // readers
    cand_rows = candidates.shape[0] * head_group
    per_request = cand_rows // requests
    history = max_pages * page_len
    score_scale = 1.0 / math.sqrt(head_dim)

    flat_ids = page_lists.reshape(slot_count)
    slot_owner = flat_ids // pages_here
    local_ids = flat_ids % pages_here
    slot_order = jnp.arange(slot_count)
    earlier_same = (slot_owner[None, :] == slot_owner[:, None]) & (
        slot_order[None, :] < slot_order[:, None]
    )
    slot_rank = jnp.sum(earlier_same.astype(jnp.int32), axis=1)
    places = slot_owner * capacity + slot_rank
    matches = places[None, :] == jnp.arange(readers * capacity)[:, None]
    asked = jnp.sum(jnp.where(matches, local_ids[None, :], 0), axis=1)
    wanted = lax.all_to_all(
        asked.reshape(readers, capacity), "pages", split_axis=0, concat_axis=0, tiled=True
    ).reshape(readers * capacity)

    histories = []
    for layer_index in range(layers):
        sent = jnp.take(page_cache[layer_index, :, 0], wanted, axis=0)
        if histories:
            sent, histories[-1] = lax.optimization_barrier((sent, histories[-1]))
        histories.append(
            lax.all_to_all(
                sent.reshape((readers, capacity) + sent.shape[1:]),
                "pages",
                split_axis=0,
                concat_axis=0,
                tiled=True,
            )
        )

    divisors = (hist_len + 1).astype(jnp.float32)
    cand_divisors = jnp.repeat(divisors, per_request)
    live = jnp.arange(history)[None, :] < hist_len[:, None]
    hidden_rows = candidates
    for layer_index in range(layers):
        weights_in = in_weight[layer_index].reshape(model_width, 4 * head_dim)
        ready = layer_norm(gather_rows(hidden_rows).astype(jnp.float32)).astype(jnp.bfloat16)
        projected = jax.nn.silu(jnp.dot(ready, weights_in, preferred_element_type=jnp.float32))
        gate_part = projected[:, :head_dim]
        value_part = projected[:, head_dim : 2 * head_dim].astype(jnp.bfloat16)
        query_part = projected[:, 2 * head_dim : 3 * head_dim].astype(jnp.bfloat16)
        key_part = projected[:, 3 * head_dim :].astype(jnp.bfloat16)
        got, query_part = lax.optimization_barrier((histories[layer_index], query_part))
        got = got.reshape(readers * capacity, 2, page_len, head_dim)
        listed = jnp.take(got, places, axis=0).reshape(requests, max_pages, 2, page_len, head_dim)
        hist_keys = listed[:, :, 0].reshape(requests, history, head_dim)
        hist_values = listed[:, :, 1].reshape(requests, history, head_dim)
        queries = query_part.reshape(requests, per_request, head_dim)
        scores = (
            jnp.einsum("rqd,rtd->rqt", queries, hist_keys, preferred_element_type=jnp.float32)
            * score_scale
        )
        weights = (
            jnp.where(live[:, None, :], jax.nn.silu(scores), 0.0) / divisors[:, None, None]
        ).astype(jnp.bfloat16)
        attended = jnp.einsum(
            "rqt,rtd->rqd", weights, hist_values, preferred_element_type=jnp.float32
        ).reshape(cand_rows, head_dim)
        self_score = (
            jnp.sum(query_part.astype(jnp.float32) * key_part.astype(jnp.float32), -1) * score_scale
        )
        self_weight = (jax.nn.silu(self_score) / cand_divisors).astype(jnp.bfloat16)
        attended = attended + self_weight.astype(jnp.float32)[:, None] * value_part.astype(
            jnp.float32
        )
        gated_rows = (layer_norm(attended) * gate_part).astype(jnp.bfloat16)
        weights_out = out_weight[layer_index].reshape(head_dim, model_width)
        terms = jnp.dot(gated_rows, weights_out, preferred_element_type=jnp.float32)
        summed = scatter_sum(terms.astype(jnp.bfloat16))
        hidden_rows = (hidden_rows.astype(jnp.float32) + summed).astype(jnp.bfloat16)
    return hidden_rows


def solution(mesh):
    in_specs = (
        P(("pages", "heads"), None),
        P(None, None, "heads", None),
        P(None, "heads", None, None),
        P(None, "pages", "heads", None, None, None),
        P("pages", None),
        P("pages"),
    )
    out_specs = P(("pages", "heads"), None)
    return jax.shard_map(
        on_device, mesh=mesh, in_specs=in_specs, out_specs=out_specs, check_vma=False
    )
```

time: 599 us -> 486 us (0.81)
  waiting for transfers between devices: 449 us -> 402 us
  other arithmetic: 39.9 us -> 14 us
  starting transfers between devices: 44.2 us -> 27.1 us
  local copies, waits for them, and re-layouts: 29.2 us -> 13.1 us
  matrix products: 20.9 us -> 14.5 us
    all_to_all x5 -> x3, waiting for transfers between devices: 141 us -> 7.84 us  [the longest x1 7.83 us: on_device(): lax.all_to_all(asked.reshape(readers, capacity), 'pages', split_axis=0, c...]
    all_gather x2, waiting for transfers between devices: 122 us -> 175 us  [gather_rows(): return lax.all_gather(rows, 'heads', axis=0, tiled=True)]
    reduce_scatter x2, waiting for transfers between devices: 185 us -> 219 us  [scatter_sum(): lax.psum_scatter(terms, 'heads', scatter_dimension=0, tiled=True)]
    all_to_all x5 -> x3, starting transfers between devices: 43.8 us -> 26.7 us  [the longest x1 13.5 us: on_device(): lax.all_to_all(asked.reshape(readers, capacity), 'pages', split_axis=0, c...]
    select_n x12 -> x6, other arithmetic: 21.3 us -> 4.36 us  [the longest x2 4.02 us: on_device(): sent = jnp.take(page_cache[layer_index, :, 0], wanted, axis=0)]
    gather x11 -> x4, local copies, waits for them, and re-layouts: 17.9 us -> 5.77 us  [the longest x2 4.27 us: on_device(): sent = jnp.take(page_cache[layer_index, :, 0], wanted, axis=0)]
    dot_general x4, matrix products: 13.6 us -> 6.8 us  [the longest x2 5.55 us: on_device(): terms = jnp.dot(gated_rows, weights_out, preferred_element_type=jnp.float32)]
  transfers between devices with their start and end apart: 9 -> 7, of which waited for: 8 -> 5; matrix products, arithmetic and copies ran while one was open for 7% -> 3% of each run, Pallas kernels for 0% -> 0%
where the time goes in v1:
time: 486 us; the launch traced here: 485 us
  waiting for transfers between devices  402 us (83%)
  starting transfers between devices  27.1 us (6%)
  matrix products  14.5 us (3%)
  other arithmetic  14 us (3%)
  between operations  13.5 us (3%)
  local copies, waits for them, and re-layouts  13.1 us (3%)
    reduce_scatter x2, waiting for transfers between devices, scatter_sum(): lax.psum_scatter(terms, 'heads', scatter_dimension=0, tiled=True)  219 us
    all_gather x2, waiting for transfers between devices, gather_rows(): return lax.all_gather(rows, 'heads', axis=0, tiled=True)  175 us
    all_to_all x1, starting transfers between devices, on_device(): lax.all_to_all(asked.reshape(readers, capacity), 'pages', split_axis=0, c...  13.5 us
    all_to_all x2, starting transfers between devices, on_device(): lax.all_to_all(sent.reshape((readers, capacity) + sent.shape[1:]), 'pages...  13.2 us
  transfers between devices with their start and end apart: 7, of which 5 were waited for; matrix products, arithmetic and copies ran while one was open for 3% of the time, Pallas kernels for 0%

profile of v1, /device:TPU:6, one launch (start us, length us, event | category | flops | bytes accessed | tf_op | source)
XLA Modules:
  0.0 484.7 jit_solution(15698231655504196997)
XLA Ops:
  6.5 0.8 copy.31
  7.7 0.8 all_to_all.12
  8.5 13.5 %all-to-all-start = ((s32[64,1,2]{2,1,0:T(1,128)}), s32[64,1,2]{2,1,0:T(1,128)S(1)}, u32[]{:S(2)}, u32[]{:S(2)}) async-start(s32[64,1,2]{2,1,0:T(1,128)} %bitcast), calls=%async_computation | async-start | bytes 65536 | tf_op jit(solution)/shard_map/all_to_all | solution.py:53
  22.0 2.0 slice_bitcast_fusion
  24.0 7.8 %all-to-all-done = s32[64,1,2]{2,1,0:T(1,128)S(1)} async-done(((s32[64,1,2]{2,1,0:T(1,128)}), s32[64,1,2]{2,1,0:T(1,128)S(1)}, u32[]{:S(2)}, u32[]{:S(2)}) %all-to-all-start) | async-done | bytes 544 | tf_op jit(solution)/shard_map/all_to_all | solution.py:53
  32.3 0.7 reduce.3
  33.2 2.2 gather_fusion
  35.4 2.1 gather_fusion.1
  37.5 4.0 broadcast_select_fusion
  41.5 4.8 all-to-all-start.1
  46.4 0.7 all-gather.3.cloned.1.call-update
  47.4 103.7 %all-gather.3.cloned.1.call-done = bf16[768,1024]{1,0:T(8,128)(2,1)} async-done(((bf16[96,1024]{1,0:T(8,128)(2,1)}), bf16[768,1024]{1,0:T(8,128)(2,1)}) %all-gather.3.cloned.1.call-update) | async-done | bytes 1572880 | tf_op jit(solution)/shard_map/all_gather | solution.py:19
  151.1 1.8 convert_reduce_fusion.1
  152.9 0.6 fusion.6
  153.5 3.9 fusion.65
  157.7 0.6 copy-done.6
  158.3 0.7 gather_fusion.2
  159.3 0.6 fusion.31
  160.7 2.8 convolution_convert_fusion.1
  163.4 8.4 %all-to-all-start.2 = ((bf16[64,2,2,32,128]{4,3,2,1,0:T(8,128)(2,1)}), bf16[64,2,2,32,128]{4,3,2,1,0:T(8,128)(2,1)S(1)}, u32[]{:S(2)}, u32[]{:S(2)}) async-start(bf16[64,2,2,32,128]{4,3,2,1,0:T(8,128)(2,1)} %bitcast.12), calls=%async_computation.3 | async-start | bytes 4194304 | tf_op jit(solution)/shard_map/all_to_all | solution.py:63
  171.9 125.0 %reduce-scatter.3.cloned.1.call-done = bf16[96,1024]{1,0:T(8,128)(2,1)} async-done(((bf16[768,1024]{1,0:T(8,128)(2,1)}), bf16[96,1024]{1,0:T(8,128)(2,1)}) %reduce-scatter.3.cloned.1.call-update) | async-done | bytes 196624 | tf_op jit(solution)/shard_map/reduce_scatter | solution.py:23
  296.9 1.7 add_convert_fusion.1
  298.8 71.7 %all-gather.5.cloned.1.call-done = bf16[768,1024]{1,0:T(8,128)(2,1)} async-done(((bf16[96,1024]{1,0:T(8,128)(2,1)}), bf16[768,1024]{1,0:T(8,128)(2,1)}) %all-gather.5.cloned.1.call-update) | async-done | bytes 1572880 | tf_op jit(solution)/shard_map/all_gather | solution.py:19
  370.4 1.8 convert_reduce_fusion
  372.3 0.6 fusion.4
  372.9 3.9 fusion.66
  377.0 0.6 copy-done.4
  377.6 0.7 gather_fusion.3
  378.7 0.6 fusion.30
  380.0 2.8 convolution_convert_fusion
  382.8 93.6 %reduce-scatter.5.cloned.1.call-done = bf16[96,1024]{1,0:T(8,128)(2,1)} async-done(((bf16[768,1024]{1,0:T(8,128)(2,1)}), bf16[96,1024]{1,0:T(8,128)(2,1)}) %reduce-scatter.5.cloned.1.call-update) | async-done | bytes 196624 | tf_op jit(solution)/shard_map/reduce_scatter | solution.py:23
  476.5 1.7 add_convert_fusion
  (73 shorter events, 4.2 us)
Async XLA Ops:
  8.5 23.3 %all-to-all-start = ((s32[64,1,2]{2,1,0:T(1,128)}), s32[64,1,2]{2,1,0:T(1,128)S(1)}, u32[]{:S(2)}, u32[]{:S(2)}) async-start(s32[64,1,2]{2,1,0:T(1,128)} %bitcast), calls=%async_computation | async-start | bytes 65536 | tf_op jit(solution)/shard_map/all_to_all | solution.py:53
  35.4 2.1 copy-start
  41.5 5.6 %copy-start.11 = (s32[16]{0:T(128)S(1)}, s32[16]{0:T(128)}, u32[]{:S(2)}) copy-start(s32[16]{0:T(128)} %param.15) | copy-start | bytes 196
  41.5 115.9 %all-to-all-start.1 = ((bf16[64,2,2,32,128]{4,3,2,1,0:T(8,128)(2,1)}), bf16[64,2,2,32,128]{4,3,2,1,0:T(8,128)(2,1)S(1)}, u32[]{:S(2)}, u32[]{:S(2)}) async-start(bf16[64,2,2,32,128]{4,3,2,1,0:T(8,128)(2,1)} %bitcast.3), calls=%async_computation.1 | async-start | bytes 4194304 | tf_op jit(solution)/shard_map/all_to_all | solution.py:63
  46.4 104.7 %all-gather.3.cloned.1.call-start = ((), (), s32[]{:S(2)}) async-start(), calls=%async_computation.5 | async-start | bytes 1769472 | tf_op jit(solution)/shard_map/all_gather | solution.py:19
  47.1 249.8 %reduce-scatter.3.cloned.1.call-start = ((), (), s32[]{:S(2)}) async-start(), calls=%async_computation.6 | async-start | bytes 1769472 | tf_op jit(solution)/shard_map/reduce_scatter | solution.py:23
  151.1 1.9 copy-start.1
  157.4 0.9 copy-start.6
  159.3 1.1 copy-start.7
  159.3 1.3 copy-start.9
  163.4 133.4 %copy-start.8 = (bf16[96,1024]{1,0:T(8,128)(2,1)S(1)}, bf16[96,1024]{1,0:T(8,128)(2,1)}, u32[]{:S(2)}) copy-start(bf16[96,1024]{1,0:T(8,128)(2,1)} %param.10) | copy-start | bytes 589828
  163.4 213.3 %all-to-all-start.2 = ((bf16[64,2,2,32,128]{4,3,2,1,0:T(8,128)(2,1)}), bf16[64,2,2,32,128]{4,3,2,1,0:T(8,128)(2,1)S(1)}, u32[]{:S(2)}, u32[]{:S(2)}) async-start(bf16[64,2,2,32,128]{4,3,2,1,0:T(8,128)(2,1)} %bitcast.12), calls=%async_computation.3 | async-start | bytes 4194304 | tf_op jit(solution)/shard_map/all_to_all | solution.py:63
  171.8 198.6 %all-gather.5.cloned.1.call-start = ((), (), s32[]{:S(2)}) async-start(), calls=%async_computation.7 | async-start | bytes 1769472 | tf_op jit(solution)/shard_map/all_gather | solution.py:19
  298.5 177.9 %reduce-scatter.5.cloned.1.call-start = ((), (), s32[]{:S(2)}) async-start(), calls=%async_computation.8 | async-start | bytes 1769472 | tf_op jit(solution)/shard_map/reduce_scatter | solution.py:23
  370.4 1.9 copy-start.2
  376.7 0.9 copy-start.4
  378.7 1.1 copy-start.5
  378.7 1.3 copy-start.10
  380.0 96.5 %copy-start.3 = (bf16[96,1024]{1,0:T(8,128)(2,1)S(1)}, bf16[96,1024]{1,0:T(8,128)(2,1)}, u32[]{:S(2)}) copy-start(bf16[96,1024]{1,0:T(8,128)(2,1)} %add_convert_fusion.1) | copy-start | bytes 589828
Sparse Core Ops, SparseCore 0:
  50.3 100.6 all-gather.2
  163.6 133.2 reduce-scatter.2
  300.0 70.3 all-gather.4
  383.0 93.4 reduce-scatter.4

commit v2 on v1

--- a/solution.py
+++ b/solution.py
@@ -1,8 +1,11 @@
+import functools
 import math
 
 import jax
 import jax.numpy as jnp
 from jax import lax
+from jax.experimental import pallas as pl
+from jax.experimental.pallas import tpu as pltpu
 from jax.sharding import PartitionSpec as P
 
 eps = 1e-05
@@ -15,12 +18,247 @@
     return centred * lax.rsqrt(spread + eps)
 
 
-def gather_rows(rows):
-    return lax.all_gather(rows, "heads", axis=0, tiled=True)
-
-
-def scatter_sum(terms):
-    return lax.psum_scatter(terms, "heads", scatter_dimension=0, tiled=True).astype(jnp.float32)
+X_SIZE = 4
+Z_LO = 4
+Z_SIZE = 8
+CORES = 2
+STRIDE = 2
+
+
+def heads_index(x_pos, z_hi):
+    return lax.rem(x_pos + X_SIZE, X_SIZE) * 2 + z_hi
+
+
+def neighbours():
+    page, head = lax.axis_index("pages"), lax.axis_index("heads")
+    x_pos, z_hi = head // 2, lax.rem(head, 2)
+    column = page // (Z_LO * CORES)
+    z_lo, core = lax.rem(page // CORES, Z_LO), lax.rem(page, CORES)
+
+    def at_z(step):
+        z_pos = lax.rem(z_hi * Z_LO + z_lo + step + Z_SIZE, Z_SIZE)
+        return ((column * Z_LO + lax.rem(z_pos, Z_LO)) * CORES + core, x_pos * 2 + z_pos // Z_LO)
+
+    return dict(
+        x=x_pos,
+        z=z_hi,
+        right=(page, heads_index(x_pos + 1, z_hi)),
+        left=(page, heads_index(x_pos - 1, z_hi)),
+        up=at_z(STRIDE),
+        down=at_z(-STRIDE),
+    )
+
+
+def greet(near):
+    barrier = pltpu.get_barrier_semaphore()
+    partners = [near[side] for side in ("right", "left", "up", "down")]
+    for partner in partners:
+        pl.semaphore_signal(
+            barrier, inc=1, device_id=partner, device_id_type=pl.DeviceIdType.MESH
+        )
+    pl.semaphore_wait(barrier, len(partners))
+
+
+def remote(source, target, sems, place, device):
+    return pltpu.make_async_remote_copy(
+        src_ref=source,
+        dst_ref=target,
+        send_sem=sems.at[(0,) + place],
+        recv_sem=sems.at[(1,) + place],
+        device_id=device,
+        device_id_type=pl.DeviceIdType.MESH,
+    )
+
+
+def wide(ref_block):
+    return ref_block.astype(jnp.float32)
+
+
+def z_relay(near, relay, z_sems, goal):
+    started = []
+    for half, (ahead, behind) in enumerate((("up", "down"), ("down", "up"))):
+        remote(relay.at[half], relay.at[half], z_sems, (0, half), near[behind]).wait_recv()
+        leg = remote(relay.at[half], goal(near[ahead], half), z_sems, (1, half), near[ahead])
+        leg.start()
+        started.append(leg)
+    return started
+
+
+def gather_phase(near, own, out, relay, z_sems, x_sems, f_sems):
+    x_pos, z_hi = near["x"], near["z"]
+    mine = heads_index(x_pos, z_hi)
+    started = []
+
+    def send(copy):
+        copy.start()
+        started.append(copy)
+
+    def spread(source, slot, level, half):
+        for side, name in (((0, "right"), (1, "left")) if half == 0 else ((1, "left"), (0, "right"))):
+            send(remote(source, out.at[slot, half], x_sems, (side, level, half), near[name]))
+
+    def pass_on(level, z_of):
+        for side, (ahead, step) in enumerate((("right", -1), ("left", 1))):
+            block = out.at[heads_index(x_pos + step, z_of), side]
+            remote(block, block, x_sems, (side, level, side), near[ahead]).wait_recv()
+            send(remote(block, block, f_sems, (side, level), near[ahead]))
+
+    for half, ahead in enumerate(("up", "down")):
+        send(remote(own.at[half], relay.at[half], z_sems, (0, half), near[ahead]))
+    for half in range(2):
+        spread(own.at[half], mine, 0, half)
+    out[mine] = own[...]
+    pass_on(0, z_hi)
+
+    def goal(device, half):
+        return out.at[heads_index(x_pos, 1 - lax.rem(device[1], 2)), half]
+
+    started += z_relay(near, relay, z_sems, goal)
+    theirs = heads_index(x_pos, 1 - z_hi)
+    for half, behind in enumerate(("down", "up")):
+        block = out.at[theirs, half]
+        remote(block, block, z_sems, (1, half), near[behind]).wait_recv()
+        spread(block, theirs, 1, half)
+    pass_on(1, 1 - z_hi)
+    for level, z_of in ((0, z_hi), (1, 1 - z_hi)):
+        for side, (ahead, step) in enumerate((("right", -1), ("left", 1))):
+            block = out.at[heads_index(x_pos + step, z_of), 1 - side]
+            remote(block, block, x_sems, (side, level, 1 - side), near[ahead]).wait_recv()
+            block = out.at[heads_index(x_pos + 2, z_of), side]
+            remote(block, block, f_sems, (side, level), near[ahead]).wait_recv()
+    for copy in started:
+        copy.wait_send()
+
+
+def reduce_phase(near, terms, first, direct, joined, joined_in, z_out, relay, z_in, z_sems, x_sems):
+    x_pos, z_hi = near["x"], near["z"]
+    z_of = (1 - z_hi, z_hi)
+    ways = ("right", "left")
+    steps = (1, -1)
+    started = []
+
+    def send(copy):
+        copy.start()
+        started.append(copy)
+
+    def far(level):
+        for side in range(2):
+            block = terms.at[heads_index(x_pos + 2, z_of[level]), side]
+            send(remote(block, first.at[level, side], x_sems, (0, level, side), near[ways[side]]))
+
+    def near_by(level):
+        for side in range(2):
+            block = terms.at[heads_index(x_pos + steps[side], z_of[level]), 1 - side]
+            send(remote(block, direct.at[level, side], x_sems, (1, level, side), near[ways[side]]))
+
+    def join(level):
+        for side in range(2):
+            here = first.at[level, side]
+            remote(here, here, x_sems, (0, level, side), near[ways[side]]).wait_recv()
+            own = terms[heads_index(x_pos + steps[side], z_of[level]), side]
+            joined[level, side] = (wide(own) + wide(here[...])).astype(jnp.bfloat16)
+            send(
+                remote(
+                    joined.at[level, side],
+                    joined_in.at[level, side],
+                    x_sems,
+                    (2, level, side),
+                    near[ways[side]],
+                )
+            )
+
+    def total(level, half):
+        here = joined_in.at[level, half]
+        remote(here, here, x_sems, (2, level, half), near[ways[half]]).wait_recv()
+        other = direct.at[level, 1 - half]
+        remote(other, other, x_sems, (1, level, 1 - half), near[ways[1 - half]]).wait_recv()
+        own = terms[heads_index(x_pos, z_of[level]), half]
+        return wide(own) + wide(here[...]) + wide(other[...])
+
+    far(0)
+    near_by(0)
+    far(1)
+    join(0)
+    near_by(1)
+    join(1)
+    for half, ahead in enumerate(("up", "down")):
+        z_out[half] = total(0, half).astype(jnp.bfloat16)
+        send(remote(z_out.at[half], relay.at[half], z_sems, (0, half), near[ahead]))
+    sums = [total(1, half) for half in range(2)]
+    started += z_relay(near, relay, z_sems, lambda device, half: z_in.at[half])
+    for half, behind in enumerate(("down", "up")):
+        here = z_in.at[half]
+        remote(here, here, z_sems, (1, half), near[behind]).wait_recv()
+        sums[half] = sums[half] + wide(here[...])
+    for copy in started:
+        copy.wait_send()
+    return sums
+
+
+def gather_kernel(own, out, *scratch):
+    near = neighbours()
+    greet(near)
+    gather_phase(near, own, out, *scratch)
+
+
+def reduce_kernel(terms, hidden, new_hidden, *scratch):
+    near = neighbours()
+    greet(near)
+    sums = reduce_phase(near, terms, *scratch)
+    for half in range(2):
+        new_hidden[half] = (wide(hidden[half]) + sums[half]).astype(jnp.bfloat16)
+
+
+def reduce_gather_kernel(split, terms, hidden, new_hidden, out, own, *scratch):
+    near = neighbours()
+    greet(near)
+    sums = reduce_phase(near, terms, *scratch[:split])
+    for half in range(2):
+        rounded = (wide(hidden[half]) + sums[half]).astype(jnp.bfloat16)
+        new_hidden[half] = rounded
+        own[half] = layer_norm(wide(rounded)).astype(jnp.bfloat16)
+    gather_phase(near, own, out, *scratch[split:])
+
+
+def exchange(hidden, terms, gather, collective_id):
+    rows, width = hidden.shape
+    group = lax.axis_size("heads")
+    half_rows = rows // 2
+    halves = (half_rows, width)
+    block = pltpu.VMEM((2,) + halves, jnp.bfloat16)
+    pair = pltpu.VMEM((2, 2) + halves, jnp.bfloat16)
+    gathering = [
+        block,
+        pltpu.SemaphoreType.DMA((2, 2, 2)),
+        pltpu.SemaphoreType.DMA((2, 2, 2, 2)),
+        pltpu.SemaphoreType.DMA((2, 2, 2)),
+    ]
+    reducing = [pair, pair, pair, pair, block, block, block]
+    reducing += [pltpu.SemaphoreType.DMA((2, 2, 2)), pltpu.SemaphoreType.DMA((2, 3, 2, 2))]
+    one = jax.ShapeDtypeStruct((2,) + halves, jnp.bfloat16)
+    whole = jax.ShapeDtypeStruct((group, 2) + halves, jnp.bfloat16)
+    if terms is None:
+        kernel, shapes, scratch = gather_kernel, [whole], gathering
+        given = [layer_norm(hidden.astype(jnp.float32)).astype(jnp.bfloat16).reshape(one.shape)]
+    else:
+        given = [terms.reshape(whole.shape), hidden.reshape(one.shape)]
+        if gather:
+            kernel = functools.partial(reduce_gather_kernel, len(reducing))
+            shapes, scratch = [one, whole], [block] + reducing + gathering
+        else:
+            kernel, shapes, scratch = reduce_kernel, [one], reducing
+    in_vmem = pl.BlockSpec(memory_space=pltpu.VMEM)
+    results = pl.pallas_call(
+        kernel,
+        out_shape=shapes,
+        in_specs=[in_vmem] * len(given),
+        out_specs=[in_vmem] * len(shapes),
+        scratch_shapes=scratch,
+        compiler_params=pltpu.CompilerParams(collective_id=collective_id, has_side_effects=True),
+    )(*given)
+    new_hidden = hidden if terms is None else results[0].reshape(rows, width)
+    ready = results[-1].reshape(group * rows, width) if gather else None
+    return new_hidden, ready
 
 
 def on_device(candidates, in_weight, out_weight, page_cache, page_lists, hist_len):
@@ -72,10 +310,9 @@
     divisors = (hist_len + 1).astype(jnp.float32)
     cand_divisors = jnp.repeat(divisors, per_request)
     live = jnp.arange(history)[None, :] < hist_len[:, None]
-    hidden_rows = candidates
+    hidden_rows, ready = exchange(candidates, None, True, 0)
     for layer_index in range(layers):
         weights_in = in_weight[layer_index].reshape(model_width, 4 * head_dim)
-        ready = layer_norm(gather_rows(hidden_rows).astype(jnp.float32)).astype(jnp.bfloat16)
         projected = jax.nn.silu(jnp.dot(ready, weights_in, preferred_element_type=jnp.float32))
         gate_part = projected[:, :head_dim]
         value_part = projected[:, head_dim : 2 * head_dim].astype(jnp.bfloat16)
@@ -107,8 +344,9 @@
         gated_rows = (layer_norm(attended) * gate_part).astype(jnp.bfloat16)
         weights_out = out_weight[layer_index].reshape(head_dim, model_width)
         terms = jnp.dot(gated_rows, weights_out, preferred_element_type=jnp.float32)
-        summed = scatter_sum(terms.astype(jnp.bfloat16))
-        hidden_rows = (hidden_rows.astype(jnp.float32) + summed).astype(jnp.bfloat16)
+        hidden_rows, ready = exchange(
+            hidden_rows, terms.astype(jnp.bfloat16), layer_index + 1 < layers, layer_index + 1
+        )
     return hidden_rows
 
 

time: 486 us -> 274 us (0.56)
  waiting for transfers between devices: 402 us -> 57.3 us
  Pallas kernels: 0 us -> 143 us
  between operations: 13.5 us -> 0.34 us
  local copies, waits for them, and re-layouts: 13.1 us -> 21.2 us
  other arithmetic: 14 us -> 7.16 us
    reduce_scatter x2 -> x0, waiting for transfers between devices: 219 us -> none  [scatter_sum(): lax.psum_scatter(terms, 'heads', scatter_dimension=0, tiled=True)]
    all_gather x2 -> x0, waiting for transfers between devices: 175 us -> none  [gather_rows(): return lax.all_gather(rows, 'heads', axis=0, tiled=True)]
    pallas_call x0 -> x3, Pallas kernels: none -> 143 us  [exchange(): pl.pallas_call(kernel, out_shape=shapes, in_specs=[in_vmem] * len(given),...]
    all_to_all x2, waiting for transfers between devices: 0.01 us -> 49.4 us  [on_device(): lax.all_to_all(sent.reshape((readers, capacity) + sent.shape[1:]), 'pages...]
  transfers between devices with their start and end apart: 7 -> 3, of which waited for: 5 -> 2; matrix products, arithmetic and copies ran while one was open for 3% -> 8% of each run, Pallas kernels for 0% -> 43%
where the time goes in v2:
time: 274 us; the launch traced here: 271 us
  Pallas kernels  143 us (52%)
  waiting for transfers between devices  57.3 us (21%)
  starting transfers between devices  25.7 us (9%)
  local copies, waits for them, and re-layouts  21.2 us (8%)
  matrix products  16.9 us (6%)
  other arithmetic  7.16 us (3%)
    pallas_call x3, Pallas kernels, exchange(): pl.pallas_call(kernel, out_shape=shapes, in_specs=[in_vmem] * len(given),...  143 us
    all_to_all x2, waiting for transfers between devices, on_device(): lax.all_to_all(sent.reshape((readers, capacity) + sent.shape[1:]), 'pages...  49.4 us
    all_to_all x1, starting transfers between devices, on_device(): lax.all_to_all(asked.reshape(readers, capacity), 'pages', split_axis=0, c...  13.5 us
    all_to_all x2, starting transfers between devices, on_device(): lax.all_to_all(sent.reshape((readers, capacity) + sent.shape[1:]), 'pages...  12.2 us
    dot_general x2, matrix products, on_device(): jnp.dot(ready, weights_in, preferred_element_type=jnp.float32)  8.09 us
    all_to_all x1, waiting for transfers between devices, on_device(): lax.all_to_all(asked.reshape(readers, capacity), 'pages', split_axis=0, c...  7.83 us
    unnamed x24, local copies, waits for them, and re-layouts  6.68 us
    dot_general x2, matrix products, on_device(): terms = jnp.dot(gated_rows, weights_out, preferred_element_type=jnp.float32)  5.53 us
  transfers between devices with their start and end apart: 3, of which 2 were waited for; matrix products, arithmetic and copies ran while one was open for 8% of the time, Pallas kernels for 43%

profile of v2, /device:TPU:6, one launch (start us, length us, event | category | flops | bytes accessed | tf_op | source)
XLA Modules:
  0.0 271.2 jit_solution(727940958517672704)
XLA Ops:
  0.0 0.8 copy.31
  1.2 0.8 all_to_all.12
  1.9 13.5 %all-to-all-start = ((s32[64,1,2]{2,1,0:T(1,128)}), s32[64,1,2]{2,1,0:T(1,128)S(1)}, u32[]{:S(2)}, u32[]{:S(2)}) async-start(s32[64,1,2]{2,1,0:T(1,128)} %bitcast), calls=%async_computation | async-start | bytes 65536 | tf_op jit(solution)/shard_map/all_to_all | solution.py:291
  15.5 2.0 slice_bitcast_fusion
  17.4 7.8 %all-to-all-done = s32[64,1,2]{2,1,0:T(1,128)S(1)} async-done(((s32[64,1,2]{2,1,0:T(1,128)}), s32[64,1,2]{2,1,0:T(1,128)S(1)}, u32[]{:S(2)}, u32[]{:S(2)}) %all-to-all-start) | async-done | bytes 544 | tf_op jit(solution)/shard_map/all_to_all | solution.py:291
  25.8 0.7 reduce.3
  26.7 2.2 gather_fusion
  28.9 2.1 gather_fusion.1
  31.0 4.0 %broadcast_select_fusion = (bf16[128,2,32,128]{3,2,1,0:T(8,128)(2,1)}, bf16[128,2,32,128]{3,2,1,0:T(8,128)(2,1)}) fusion(bf16[128,2,32,128]{3,2,1,0:T(8,128)(2,1)} %gather_fusion.1, pred[128]{0:T(512)(128)(4,1)S(1)} %compare_and_fusion.1, bf16[128,2,32,128]{3,2,1,0:T(8,128)(2,1)S(1)} %copy-done), kind=kLoop, calls=%fused_computation.4 | loop fusion | flops 2097152 | bytes 8388736 | tf_op jit(solution)/shard_map/jit(_take)/select_n | solution.py:297
  35.0 4.8 %all-to-all-start.1 = ((bf16[64,2,2,32,128]{4,3,2,1,0:T(8,128)(2,1)}), bf16[64,2,2,32,128]{4,3,2,1,0:T(8,128)(2,1)S(1)}, u32[]{:S(2)}, u32[]{:S(2)}) async-start(bf16[64,2,2,32,128]{4,3,2,1,0:T(8,128)(2,1)} %bitcast.3), calls=%async_computation.1 | async-start | bytes 4194304 | tf_op jit(solution)/shard_map/all_to_all | solution.py:301
  40.2 49.4 %all-to-all-done.1 = bf16[64,2,2,32,128]{4,3,2,1,0:T(8,128)(2,1)S(1)} async-done(((bf16[64,2,2,32,128]{4,3,2,1,0:T(8,128)(2,1)}), bf16[64,2,2,32,128]{4,3,2,1,0:T(8,128)(2,1)S(1)}, u32[]{:S(2)}, u32[]{:S(2)}) %all-to-all-start.1) | async-done | bytes 2097184 | tf_op jit(solution)/shard_map/all_to_all | solution.py:301
  89.6 1.3 copy-done.1
  90.9 7.4 %all-to-all-start.2 = ((bf16[64,2,2,32,128]{4,3,2,1,0:T(8,128)(2,1)}), bf16[64,2,2,32,128]{4,3,2,1,0:T(8,128)(2,1)S(1)}, u32[]{:S(2)}, u32[]{:S(2)}) async-start(bf16[64,2,2,32,128]{4,3,2,1,0:T(8,128)(2,1)} %bitcast.4), calls=%async_computation.2 | async-start | bytes 4194304 | tf_op jit(solution)/shard_map/all_to_all | solution.py:301
  98.3 0.8 fusion.13
  99.1 70.3 %shard_map.64 = bf16[8,2,48,1024]{3,2,1,0:T(8,128)(2,1)} custom-call(bf16[2,48,1024]{2,1,0:T(8,128)(2,1)} %bitcast.70), custom_call_target="tpu_custom_call" | custom-call | tf_op jit(solution)/shard_map/pallas_call | solution.py:251
  169.4 4.1 %fusion.51 = (bf16[768,512]{0,1:T(8,128)(2,1)S(1)}, f32[768,512]{0,1:T(8,128)}) fusion(bf16[768,1024]{1,0:T(8,128)(2,1)} %bitcast.69, bf16[2,1024,1,512]{3,1,2,0:T(8,128)(2,1)} %param.11), kind=kOutput, calls=%fused_computation.99 | convolution fusion | flops 807272448 | bytes 4980736 | tf_op jit(solution)/shard_map/dot_general | solution.py:316
  173.5 0.9 copy-done.3
  174.6 0.8 copy.33
  175.5 2.3 gather_fusion.2
  178.0 1.1 fusion.50
  179.1 2.6 fusion.17
  181.7 1.2 copy.36
  183.2 0.7 copy-done.7
  184.0 2.8 %convolution_convert_fusion.1 = bf16[768,1024]{1,0:T(8,128)(2,1)} fusion(bf16[2,1,128,1024]{3,2,1,0:T(8,128)(2,1)S(1)} %copy-done.7, f32[768,512]{0,1:T(8,128)} %get-tuple-element.36, f32[768]{0:T(1024)S(1)} %add_rsqrt_fusion.1, f32[768]{0:T(1024)S(1)} %broadcast_multiply_fusion.1, f32[768,128]{0,1:T(8,128)S(1)} %copy.36, ...), kind=kOutput, calls=%fused_computation.7 | convolution fusion | flops 202801152 | bytes 2830336 | tf_op jit(solution)/shard_map/dot_general | solution.py:346
  186.7 46.9 %shard_map.65 = (bf16[2,48,1024]{2,1,0:T(8,128)(2,1)}, bf16[8,2,48,1024]{3,2,1,0:T(8,128)(2,1)}) custom-call(bf16[8,2,48,1024]{3,2,1,0:T(8,128)(2,1)} %bitcast.62, bf16[2,48,1024]{2,1,0:T(8,128)(2,1)} %bitcast.68), custom_call_target="tpu_custom_call" | custom-call | tf_op jit(solution)/shard_map/pallas_call | solution.py:251
  233.6 4.0 %fusion.52 = (bf16[768,512]{0,1:T(8,128)(2,1)S(1)}, f32[768,512]{0,1:T(8,128)}) fusion(bf16[768,1024]{1,0:T(8,128)(2,1)} %bitcast.80, bf16[2,1024,1,512]{3,1,2,0:T(8,128)(2,1)} %param.11), kind=kOutput, calls=%fused_computation.100 | convolution fusion | flops 807272448 | bytes 4980736 | tf_op jit(solution)/shard_map/dot_general | solution.py:316
  238.0 0.6 copy-done.5
  238.6 0.7 gather_fusion.3
  239.6 0.6 fusion.16
  241.4 2.8 %convolution_convert_fusion = bf16[768,1024]{1,0:T(8,128)(2,1)} fusion(bf16[2,1,128,1024]{3,2,1,0:T(8,128)(2,1)S(1)} %copy-done.8, f32[768,512]{0,1:T(8,128)} %get-tuple-element.38, f32[768]{0:T(1024)S(1)} %add_rsqrt_fusion, f32[768]{0:T(1024)S(1)} %broadcast_multiply_fusion, f32[768,128]{0,1:T(8,128)S(1)} %copy.40, bf16[768,512]{0,1:T(8,128)(2,1)S(1)} %copy-done.6, ...), kind=kOutput, calls=%fused_computation.6 | convolution fusion | flops 202801152 | bytes 2830336 | tf_op jit(solution)/shard_map/dot_general | solution.py:346
  244.1 25.5 %shard_map.66 = bf16[2,48,1024]{2,1,0:T(8,128)(2,1)} custom-call(bf16[8,2,48,1024]{3,2,1,0:T(8,128)(2,1)} %bitcast.63, bf16[2,48,1024]{2,1,0:T(8,128)(2,1)} %get-tuple-element.22.hidden), custom_call_target="tpu_custom_call" | custom-call | tf_op jit(solution)/shard_map/pallas_call | solution.py:251
  269.6 1.6 copy.46
  (58 shorter events, 3.7 us)
Async XLA Ops:
  1.9 23.3 %all-to-all-start = ((s32[64,1,2]{2,1,0:T(1,128)}), s32[64,1,2]{2,1,0:T(1,128)S(1)}, u32[]{:S(2)}, u32[]{:S(2)}) async-start(s32[64,1,2]{2,1,0:T(1,128)} %bitcast), calls=%async_computation | async-start | bytes 65536 | tf_op jit(solution)/shard_map/all_to_all | solution.py:291
  28.9 2.1 copy-start
  35.0 4.8 %copy-start.2 = (bf16[96,1024]{1,0:T(8,128)(2,1)S(1)}, bf16[96,1024]{1,0:T(8,128)(2,1)}, u32[]{:S(2)}) copy-start(bf16[96,1024]{1,0:T(8,128)(2,1)} %param.10) | copy-start | bytes 589828
  35.0 54.6 %all-to-all-start.1 = ((bf16[64,2,2,32,128]{4,3,2,1,0:T(8,128)(2,1)}), bf16[64,2,2,32,128]{4,3,2,1,0:T(8,128)(2,1)S(1)}, u32[]{:S(2)}, u32[]{:S(2)}) async-start(bf16[64,2,2,32,128]{4,3,2,1,0:T(8,128)(2,1)} %bitcast.3), calls=%async_computation.1 | async-start | bytes 4194304 | tf_op jit(solution)/shard_map/all_to_all | solution.py:301
  89.6 1.3 copy-start.1
  90.9 146.8 %all-to-all-start.2 = ((bf16[64,2,2,32,128]{4,3,2,1,0:T(8,128)(2,1)}), bf16[64,2,2,32,128]{4,3,2,1,0:T(8,128)(2,1)S(1)}, u32[]{:S(2)}, u32[]{:S(2)}) async-start(bf16[64,2,2,32,128]{4,3,2,1,0:T(8,128)(2,1)} %bitcast.4), calls=%async_computation.2 | async-start | bytes 4194304 | tf_op jit(solution)/shard_map/all_to_all | solution.py:301
  169.4 5.0 %copy-start.10 = (s32[16]{0:T(128)S(1)}, s32[16]{0:T(128)}, u32[]{:S(2)}) copy-start(s32[16]{0:T(128)} %param.15) | copy-start | bytes 196
  173.5 0.9 copy-start.3
  178.0 1.1 copy-start.9
  179.1 3.8 %copy-start.4 = (bf16[768,512]{0,1:T(8,128)(2,1)S(1)}, bf16[768,512]{0,1:T(8,128)(2,1)}, u32[]{:S(2)}) copy-start(bf16[768,512]{0,1:T(8,128)(2,1)} %copy-done.3) | copy-start | bytes 2359300
  182.9 1.0 copy-start.7
  237.7 0.9 copy-start.5
  239.6 1.1 copy-start.6
  240.2 1.1 copy-start.8

commit v3 on v2

--- a/solution.py
+++ b/solution.py
@@ -292,25 +292,17 @@
         asked.reshape(readers, capacity), "pages", split_axis=0, concat_axis=0, tiled=True
     ).reshape(readers * capacity)
 
-    histories = []
-    for layer_index in range(layers):
-        sent = jnp.take(page_cache[layer_index, :, 0], wanted, axis=0)
-        if histories:
-            sent, histories[-1] = lax.optimization_barrier((sent, histories[-1]))
-        histories.append(
-            lax.all_to_all(
-                sent.reshape((readers, capacity) + sent.shape[1:]),
-                "pages",
-                split_axis=0,
-                concat_axis=0,
-                tiled=True,
-            )
-        )
-
+    def history_of(layer_index, after):
+        rows = page_cache.at[layer_index, wanted, 0].get(mode="promise_in_bounds")
+        rows, after = lax.optimization_barrier((rows, after))
+        rows = rows.reshape((readers, capacity) + rows.shape[1:])
+        return lax.all_to_all(rows, "pages", split_axis=0, concat_axis=0, tiled=True), after
+
+    hidden_rows, ready = exchange(candidates, None, True, 0)
+    history_now, ready = history_of(0, ready)
     divisors = (hist_len + 1).astype(jnp.float32)
     cand_divisors = jnp.repeat(divisors, per_request)
     live = jnp.arange(history)[None, :] < hist_len[:, None]
-    hidden_rows, ready = exchange(candidates, None, True, 0)
     for layer_index in range(layers):
         weights_in = in_weight[layer_index].reshape(model_width, 4 * head_dim)
         projected = jax.nn.silu(jnp.dot(ready, weights_in, preferred_element_type=jnp.float32))
@@ -318,9 +310,11 @@
         value_part = projected[:, head_dim : 2 * head_dim].astype(jnp.bfloat16)
         query_part = projected[:, 2 * head_dim : 3 * head_dim].astype(jnp.bfloat16)
         key_part = projected[:, 3 * head_dim :].astype(jnp.bfloat16)
-        got, query_part = lax.optimization_barrier((histories[layer_index], query_part))
+        if layer_index + 1 < layers:
+            history_next, query_part = history_of(layer_index + 1, query_part)
+        got, query_part = lax.optimization_barrier((history_now, query_part))
         got = got.reshape(readers * capacity, 2, page_len, head_dim)
-        listed = jnp.take(got, places, axis=0).reshape(requests, max_pages, 2, page_len, head_dim)
+        listed = got.at[places].get(mode="promise_in_bounds").reshape(requests, max_pages, 2, page_len, head_dim)
         hist_keys = listed[:, :, 0].reshape(requests, history, head_dim)
         hist_values = listed[:, :, 1].reshape(requests, history, head_dim)
         queries = query_part.reshape(requests, per_request, head_dim)
@@ -347,6 +341,7 @@
         hidden_rows, ready = exchange(
             hidden_rows, terms.astype(jnp.bfloat16), layer_index + 1 < layers, layer_index + 1
         )
+        history_now = history_next
     return hidden_rows
 
 

time: 274 us -> 249 us (0.909)
  Pallas kernels: 143 us -> 128 us
  waiting for transfers between devices: 57.3 us -> 42.7 us
  starting transfers between devices: 25.7 us -> 31.1 us
    pallas_call x3, Pallas kernels: 143 us -> 128 us  [exchange(): pl.pallas_call(kernel, out_shape=shapes, in_specs=[in_vmem] * len(given),...]
    all_to_all x1, waiting for transfers between devices: 7.83 us -> 0.01 us  [on_device(): lax.all_to_all(asked.reshape(readers, capacity), 'pages', split_axis=0, c...]
    all_to_all x2, waiting for transfers between devices: 49.4 us -> 42.7 us  [history_of(): lax.all_to_all(rows, 'pages', split_axis=0, concat_axis=0, tiled=True)]
    all_to_all x2, starting transfers between devices: 12.2 us -> 17.5 us  [history_of(): lax.all_to_all(rows, 'pages', split_axis=0, concat_axis=0, tiled=True)]
    select_n x5 -> x1, other arithmetic: 4.35 us -> 0.01 us  [on_device(): got.at[places].get(mode='promise_in_bounds')]
    unnamed x24 -> x16, local copies, waits for them, and re-layouts: 6.68 us -> 4.84 us
  transfers between devices with their start and end apart: 3 -> 3, of which waited for: 2 -> 1; matrix products, arithmetic and copies ran while one was open for 8% -> 10% of each run, Pallas kernels for 43% -> 41%
where the time goes in v3:
time: 249 us; the launch traced here: 247 us
  Pallas kernels  128 us (51%)
  waiting for transfers between devices  42.7 us (17%)
  starting transfers between devices  31.1 us (12%)
  local copies, waits for them, and re-layouts  20.7 us (8%)
  matrix products  19 us (8%)
  other arithmetic  5.62 us (2%)
    pallas_call x3, Pallas kernels, exchange(): pl.pallas_call(kernel, out_shape=shapes, in_specs=[in_vmem] * len(given),...  128 us
    all_to_all x2, waiting for transfers between devices, history_of(): lax.all_to_all(rows, 'pages', split_axis=0, concat_axis=0, tiled=True)  42.7 us
    all_to_all x2, starting transfers between devices, history_of(): lax.all_to_all(rows, 'pages', split_axis=0, concat_axis=0, tiled=True)  17.5 us
    all_to_all x1, starting transfers between devices, on_device(): lax.all_to_all(asked.reshape(readers, capacity), 'pages', split_axis=0, c...  13.5 us
    dot_general x2, matrix products, on_device(): jnp.dot(ready, weights_in, preferred_element_type=jnp.float32)  8.08 us
    dot_general x2, matrix products, on_device(): terms = jnp.dot(gated_rows, weights_out, preferred_element_type=jnp.float32)  5.63 us
    dot_general x2, matrix products, on_device(): jnp.einsum('rqt,rtd->rqd', weights, hist_values, preferred_element_type=j...  5.27 us
  transfers between devices with their start and end apart: 3, of which 1 were waited for; matrix products, arithmetic and copies ran while one was open for 10% of the time, Pallas kernels for 41%

profile of v3, /device:TPU:6, one launch (start us, length us, event | category | flops | bytes accessed | tf_op | source)
XLA Modules:
  0.0 247.5 jit_solution(13520613037608323053)
XLA Ops:
  0.0 0.9 copy.34
  1.3 0.7 all_to_all.12
  2.1 13.5 %all-to-all-start = ((s32[64,1,2]{2,1,0:T(1,128)}), s32[64,1,2]{2,1,0:T(1,128)S(1)}, u32[]{:S(2)}, u32[]{:S(2)}) async-start(s32[64,1,2]{2,1,0:T(1,128)} %bitcast), calls=%async_computation | async-start | bytes 65536 | tf_op jit(solution)/shard_map/all_to_all | solution.py:291
  15.6 1.1 convert_reduce_fusion
  16.7 1.1 fusion.12
  17.8 1.8 fusion.13
  19.6 30.8 %shard_map.64 = bf16[8,2,48,1024]{3,2,1,0:T(8,128)(2,1)} custom-call(bf16[2,48,1024]{2,1,0:T(8,128)(2,1)} %bitcast.76), custom_call_target="tpu_custom_call" | custom-call | tf_op jit(solution)/shard_map/pallas_call | solution.py:251
  50.4 0.5 broadcast.452
  51.0 0.7 reduce.3
  51.9 2.2 gather_fusion.1
  54.1 10.1 %all-to-all-start.2 = ((bf16[64,2,2,32,128]{4,3,2,1,0:T(8,128)(2,1)}), bf16[64,2,2,32,128]{4,3,2,1,0:T(8,128)(2,1)}, u32[]{:S(2)}, u32[]{:S(2)}) async-start(bf16[64,2,2,32,128]{4,3,2,1,0:T(8,128)(2,1)} %bitcast.69), calls=%async_computation.2 | async-start | bytes 4194304 | tf_op jit(solution)/shard_map/all_to_all | solution.py:299
  64.2 2.3 gather_fusion
  66.5 4.0 %fusion.55 = (bf16[768,512]{0,1:T(8,128)(2,1)S(1)}, f32[768,512]{0,1:T(8,128)}) fusion(bf16[768,1024]{1,0:T(8,128)(2,1)} %bitcast.75, bf16[2,1024,1,512]{3,1,2,0:T(8,128)(2,1)} %param.7), kind=kOutput, calls=%fused_computation.100 | convolution fusion | flops 807272448 | bytes 4980736 | tf_op jit(solution)/shard_map/dot_general | solution.py:308
  70.6 0.9 copy-done.1
  71.5 42.7 %all-to-all-done.2 = bf16[64,2,2,32,128]{4,3,2,1,0:T(8,128)(2,1)} async-done(((bf16[64,2,2,32,128]{4,3,2,1,0:T(8,128)(2,1)}), bf16[64,2,2,32,128]{4,3,2,1,0:T(8,128)(2,1)}, u32[]{:S(2)}, u32[]{:S(2)}) %all-to-all-start.2) | async-done | bytes 2097184 | tf_op jit(solution)/shard_map/all_to_all | solution.py:299
  114.3 7.4 %all-to-all-start.1 = ((bf16[64,2,2,32,128]{4,3,2,1,0:T(8,128)(2,1)}), bf16[64,2,2,32,128]{4,3,2,1,0:T(8,128)(2,1)}, u32[]{:S(2)}, u32[]{:S(2)}) async-start(bf16[64,2,2,32,128]{4,3,2,1,0:T(8,128)(2,1)} %bitcast.68), calls=%async_computation.1 | async-start | bytes 4194304 | tf_op jit(solution)/shard_map/all_to_all | solution.py:299
  122.2 2.3 gather_fusion.2
  124.5 1.1 fusion.54
  125.6 2.6 %fusion.17 = f32[16,48,128]{2,1,0:T(8,128)} fusion(bf16[16,128,128]{2,1,0:T(8,128)(2,1)} %bitcast.81, bf16[16,48,128]{2,1,0:T(8,128)(2,1)S(1)} %bitcast.85, bf16[16,128,128]{2,1,0:T(8,128)(2,1)} %bitcast.80, f32[16]{0:T(128)S(1)} %add_convert_fusion, pred[16,128]{1,0:T(8,128)(4,1)S(1)} %iota_compare_fusion.2), kind=kOutput, calls=%fused_computation.35 | convolution fusion | flops 51118080 | bytes 1640512 | tf_op jit(solution)/shard_map/rqt,rtd->rqd/dot_general | solution.py:328
  128.3 1.2 copy.40
  129.8 0.7 copy-done.5
  130.5 2.8 %convolution_convert_fusion.1 = bf16[768,1024]{1,0:T(8,128)(2,1)} fusion(bf16[2,1,128,1024]{3,2,1,0:T(8,128)(2,1)S(1)} %copy-done.5, f32[768,512]{0,1:T(8,128)} %get-tuple-element.34, f32[768]{0:T(1024)S(1)} %add_rsqrt_fusion.1, f32[768]{0:T(1024)S(1)} %broadcast_multiply_fusion.1, f32[768,128]{0,1:T(8,128)S(1)} %copy.40, ...), kind=kOutput, calls=%fused_computation.5 | convolution fusion | flops 202801152 | bytes 2830336 | tf_op jit(solution)/shard_map/dot_general | solution.py:340
  133.3 71.0 %shard_map.65 = (bf16[2,48,1024]{2,1,0:T(8,128)(2,1)}, bf16[8,2,48,1024]{3,2,1,0:T(8,128)(2,1)}) custom-call(bf16[8,2,48,1024]{3,2,1,0:T(8,128)(2,1)} %bitcast.70, bf16[2,48,1024]{2,1,0:T(8,128)(2,1)} %bitcast.74), custom_call_target="tpu_custom_call" | custom-call | tf_op jit(solution)/shard_map/pallas_call | solution.py:251
  204.3 4.1 %fusion.56 = (bf16[768,512]{0,1:T(8,128)(2,1)S(1)}, f32[768,512]{0,1:T(8,128)}) fusion(bf16[768,1024]{1,0:T(8,128)(2,1)} %bitcast.86, bf16[2,1024,1,512]{3,1,2,0:T(8,128)(2,1)} %param.7), kind=kOutput, calls=%fused_computation.101 | convolution fusion | flops 807272448 | bytes 4980736 | tf_op jit(solution)/shard_map/dot_general | solution.py:308
  208.7 0.6 copy-done.3
  209.3 2.3 gather_fusion.3
  211.6 1.1 fusion.53
  212.8 2.6 %fusion.16 = f32[16,48,128]{2,1,0:T(8,128)} fusion(bf16[16,128,128]{2,1,0:T(8,128)(2,1)} %bitcast.79, bf16[16,48,128]{2,1,0:T(8,128)(2,1)S(1)} %bitcast.84, bf16[16,128,128]{2,1,0:T(8,128)(2,1)} %bitcast.78, f32[16]{0:T(128)S(1)} %add_convert_fusion, pred[16,128]{1,0:T(8,128)(4,1)S(1)} %iota_compare_fusion.2), kind=kOutput, calls=%fused_computation.30 | convolution fusion | flops 51118080 | bytes 1640512 | tf_op jit(solution)/shard_map/rqt,rtd->rqd/dot_general | solution.py:328
  215.4 1.2 copy.44
  216.8 2.8 %convolution_convert_fusion = bf16[768,1024]{1,0:T(8,128)(2,1)} fusion(bf16[2,1,128,1024]{3,2,1,0:T(8,128)(2,1)} %param.8, f32[768,512]{0,1:T(8,128)} %get-tuple-element.36, f32[768]{0:T(1024)S(1)} %add_rsqrt_fusion, f32[768]{0:T(1024)S(1)} %broadcast_multiply_fusion, f32[768,128]{0,1:T(8,128)S(1)} %copy.44, bf16[768,512]{0,1:T(8,128)(2,1)S(1)} %copy-done.4, ...), kind=kOutput, calls=%fused_computation.4 | convolution fusion | flops 202801152 | bytes 2830336 | tf_op jit(solution)/shard_map/dot_general | solution.py:340
  219.6 26.2 %shard_map.66 = bf16[2,48,1024]{2,1,0:T(8,128)(2,1)} custom-call(bf16[8,2,48,1024]{3,2,1,0:T(8,128)(2,1)} %bitcast.71, bf16[2,48,1024]{2,1,0:T(8,128)(2,1)} %get-tuple-element.24.hidden), custom_call_target="tpu_custom_call" | custom-call | tf_op jit(solution)/shard_map/pallas_call | solution.py:251
  245.9 1.6 copy.50
  (45 shorter events, 1.8 us)
Async XLA Ops:
  0.0 51.8 %copy-start = (bf16[2,64,1,2,32,128]{5,4,3,2,1,0:T(8,128)(2,1)S(1)}, bf16[2,64,1,2,32,128]{5,4,3,2,1,0:T(8,128)(2,1)}, u32[]{:S(2)}) copy-start(bf16[2,64,1,2,32,128]{5,4,3,2,1,0:T(8,128)(2,1)} %param.9) | copy-start | bytes 6291460
  2.1 48.4 %all-to-all-start = ((s32[64,1,2]{2,1,0:T(1,128)}), s32[64,1,2]{2,1,0:T(1,128)S(1)}, u32[]{:S(2)}, u32[]{:S(2)}) async-start(s32[64,1,2]{2,1,0:T(1,128)} %bitcast), calls=%async_computation | async-start | bytes 65536 | tf_op jit(solution)/shard_map/all_to_all | solution.py:291
  54.1 60.2 %all-to-all-start.2 = ((bf16[64,2,2,32,128]{4,3,2,1,0:T(8,128)(2,1)}), bf16[64,2,2,32,128]{4,3,2,1,0:T(8,128)(2,1)}, u32[]{:S(2)}, u32[]{:S(2)}) async-start(bf16[64,2,2,32,128]{4,3,2,1,0:T(8,128)(2,1)} %bitcast.69), calls=%async_computation.2 | async-start | bytes 4194304 | tf_op jit(solution)/shard_map/all_to_all | solution.py:299
  70.6 0.9 copy-start.1
  114.2 7.5 %copy-start.6 = (s32[16]{0:T(128)S(1)}, s32[16]{0:T(128)}, u32[]{:S(2)}) copy-start(s32[16]{0:T(128)} %param.11) | copy-start | bytes 196
  114.3 94.2 %all-to-all-start.1 = ((bf16[64,2,2,32,128]{4,3,2,1,0:T(8,128)(2,1)}), bf16[64,2,2,32,128]{4,3,2,1,0:T(8,128)(2,1)}, u32[]{:S(2)}, u32[]{:S(2)}) async-start(bf16[64,2,2,32,128]{4,3,2,1,0:T(8,128)(2,1)} %bitcast.68), calls=%async_computation.1 | async-start | bytes 4194304 | tf_op jit(solution)/shard_map/all_to_all | solution.py:299
  125.6 3.8 %copy-start.2 = (bf16[768,512]{0,1:T(8,128)(2,1)S(1)}, bf16[768,512]{0,1:T(8,128)(2,1)}, u32[]{:S(2)}) copy-start(bf16[768,512]{0,1:T(8,128)(2,1)} %copy-done.1) | copy-start | bytes 2359300
  129.5 1.0 copy-start.5
  208.4 0.9 copy-start.3
  212.8 3.8 %copy-start.4 = (bf16[768,512]{0,1:T(8,128)(2,1)S(1)}, bf16[768,512]{0,1:T(8,128)(2,1)}, u32[]{:S(2)}) copy-start(bf16[768,512]{0,1:T(8,128)(2,1)} %copy-done.3) | copy-start | bytes 2359300

commit v4 on v3

--- a/solution.py
+++ b/solution.py
@@ -1,4 +1,3 @@
-import functools
 import math
 
 import jax
@@ -130,7 +129,7 @@
         copy.wait_send()
 
 
-def reduce_phase(near, terms, first, direct, joined, joined_in, z_out, relay, z_in, z_sems, x_sems):
+def sum_along_x(near, terms, first, direct, joined, joined_in, x_sems):
     x_pos, z_hi = near["x"], near["z"]
     z_of = (1 - z_hi, z_hi)
     ways = ("right", "left")
@@ -181,6 +180,16 @@
     join(0)
     near_by(1)
     join(1)
+    return total, started
+
+
+def reduce_phase(near, terms, first, direct, joined, joined_in, z_out, relay, z_in, z_sems, x_sems):
+    total, started = sum_along_x(near, terms, first, direct, joined, joined_in, x_sems)
+
+    def send(copy):
+        copy.start()
+        started.append(copy)
+
     for half, ahead in enumerate(("up", "down")):
         z_out[half] = total(0, half).astype(jnp.bfloat16)
         send(remote(z_out.at[half], relay.at[half], z_sems, (0, half), near[ahead]))
@@ -209,15 +218,62 @@
         new_hidden[half] = (wide(hidden[half]) + sums[half]).astype(jnp.bfloat16)
 
 
-def reduce_gather_kernel(split, terms, hidden, new_hidden, out, own, *scratch):
+def reduce_gather_kernel(
+    terms, hidden, new_hidden, out, first, direct, joined, joined_in,
+    z_out, relay, z_in, own, z_sems, x_sems, g_sems, f_sems
+):
     near = neighbours()
     greet(near)
-    sums = reduce_phase(near, terms, *scratch[:split])
-    for half in range(2):
-        rounded = (wide(hidden[half]) + sums[half]).astype(jnp.bfloat16)
-        new_hidden[half] = rounded
-        own[half] = layer_norm(wide(rounded)).astype(jnp.bfloat16)
-    gather_phase(near, own, out, *scratch[split:])
+    x_pos, z_hi = near["x"], near["z"]
+    z_of = (1 - z_hi, z_hi)
+    ways = (("right", -1), ("left", 1))
+    total, started = sum_along_x(near, terms, first, direct, joined, joined_in, x_sems)
+
+    def send(copy):
+        copy.start()
+        started.append(copy)
+
+    for level in range(2):
+        for half, ahead in enumerate(("up", "down")):
+            partial = total(level, half)
+            if level == 1:
+                partial = partial + wide(hidden[half])
+            z_out[level, half] = partial.astype(jnp.bfloat16)
+            place = relay.at[level, half]
+            send(remote(z_out.at[level, half], place, z_sems, (0, level, half), near[ahead]))
+    for level in range(2):
+        for half, (ahead, behind) in enumerate((("up", "down"), ("down", "up"))):
+            place = relay.at[level, half]
+            remote(place, place, z_sems, (0, level, half), near[behind]).wait_recv()
+            target = z_in.at[1 - level, half]
+            send(remote(place, target, z_sems, (1, level, half), near[ahead]))
+    for level in (1, 0):
+        slot = heads_index(x_pos, z_of[level])
+        for half, behind in enumerate(("down", "up")):
+            here = z_in.at[level, half]
+            remote(here, here, z_sems, (1, 1 - level, half), near[behind]).wait_recv()
+            rounded = (wide(z_out[level, half]) + wide(here[...])).astype(jnp.bfloat16)
+            if level == 1:
+                new_hidden[half] = rounded
+            own[level, half] = layer_norm(wide(rounded)).astype(jnp.bfloat16)
+            for side in (half, 1 - half):
+                target = out.at[slot, half]
+                device = near[ways[side][0]]
+                send(remote(own.at[level, half], target, g_sems, (side, level, half), device))
+        out[slot] = own[level]
+    for level in (1, 0):
+        for side, (ahead, step) in enumerate(ways):
+            block = out.at[heads_index(x_pos + step, z_of[level]), side]
+            remote(block, block, g_sems, (side, level, side), near[ahead]).wait_recv()
+            send(remote(block, block, f_sems, (side, level), near[ahead]))
+    for level in (1, 0):
+        for side, (ahead, step) in enumerate(ways):
+            block = out.at[heads_index(x_pos + step, z_of[level]), 1 - side]
+            remote(block, block, g_sems, (side, level, 1 - side), near[ahead]).wait_recv()
+            block = out.at[heads_index(x_pos + 2, z_of[level]), side]
+            remote(block, block, f_sems, (side, level), near[ahead]).wait_recv()
+    for copy in started:
+        copy.wait_send()
 
 
 def exchange(hidden, terms, gather, collective_id):
@@ -243,8 +299,8 @@
     else:
         given = [terms.reshape(whole.shape), hidden.reshape(one.shape)]
         if gather:
-            kernel = functools.partial(reduce_gather_kernel, len(reducing))
-            shapes, scratch = [one, whole], [block] + reducing + gathering
+            kernel, shapes = reduce_gather_kernel, [one, whole]
+            scratch = [pair] * 8 + [pltpu.SemaphoreType.DMA((2, 2, 2, 2)), reducing[-1]] + gathering[2:]
         else:
             kernel, shapes, scratch = reduce_kernel, [one], reducing
     in_vmem = pl.BlockSpec(memory_space=pltpu.VMEM)

time: 249 us -> 245 us (0.984)
  the two profiles are of different devices: /device:TPU:6 before, /device:TPU:96 now
where the time goes in v4:
time: 245 us; the launch traced here: 244 us
  Pallas kernels  127 us (52%)
  waiting for transfers between devices  39 us (16%)
  starting transfers between devices  33.2 us (14%)
  local copies, waits for them, and re-layouts  20.7 us (8%)
  matrix products  19 us (8%)
  other arithmetic  5.62 us (2%)
    pallas_call x3, Pallas kernels, exchange(): pl.pallas_call(kernel, out_shape=shapes, in_specs=[in_vmem] * len(given),...  127 us
    all_to_all x2, waiting for transfers between devices, history_of(): lax.all_to_all(rows, 'pages', split_axis=0, concat_axis=0, tiled=True)  39 us
    all_to_all x2, starting transfers between devices, history_of(): lax.all_to_all(rows, 'pages', split_axis=0, concat_axis=0, tiled=True)  20.8 us
    all_to_all x1, starting transfers between devices, on_device(): lax.all_to_all(asked.reshape(readers, capacity), 'pages', split_axis=0, c...  12.4 us
    dot_general x2, matrix products, on_device(): jnp.dot(ready, weights_in, preferred_element_type=jnp.float32)  8.08 us
    dot_general x2, matrix products, on_device(): terms = jnp.dot(gated_rows, weights_out, preferred_element_type=jnp.float32)  5.63 us
    dot_general x2, matrix products, on_device(): jnp.einsum('rqt,rtd->rqd', weights, hist_values, preferred_element_type=j...  5.27 us
  transfers between devices with their start and end apart: 3, of which 1 were waited for; matrix products, arithmetic and copies ran while one was open for 10% of the time, Pallas kernels for 40%

profile of v4, /device:TPU:96, one launch (start us, length us, event | category | flops | bytes accessed | tf_op | source)
XLA Modules:
  0.0 244.4 jit_solution(18089536782555135349)
XLA Ops:
  0.0 0.9 copy.34
  1.3 0.7 all_to_all.12
  2.1 12.4 %all-to-all-start = ((s32[64,1,2]{2,1,0:T(1,128)}), s32[64,1,2]{2,1,0:T(1,128)S(1)}, u32[]{:S(2)}, u32[]{:S(2)}) async-start(s32[64,1,2]{2,1,0:T(1,128)} %bitcast), calls=%async_computation | async-start | bytes 65536 | tf_op jit(solution)/shard_map/all_to_all | solution.py:347
  14.5 1.1 convert_reduce_fusion
  15.5 1.1 fusion.12
  16.7 1.8 fusion.13
  18.5 31.8 %shard_map.64 = bf16[8,2,48,1024]{3,2,1,0:T(8,128)(2,1)} custom-call(bf16[2,48,1024]{2,1,0:T(8,128)(2,1)} %bitcast.76), custom_call_target="tpu_custom_call" | custom-call | tf_op jit(solution)/shard_map/pallas_call | solution.py:307
  50.3 0.5 broadcast.452
  50.8 0.7 reduce.3
  51.7 2.2 gather_fusion.1
  53.9 9.8 %all-to-all-start.2 = ((bf16[64,2,2,32,128]{4,3,2,1,0:T(8,128)(2,1)}), bf16[64,2,2,32,128]{4,3,2,1,0:T(8,128)(2,1)}, u32[]{:S(2)}, u32[]{:S(2)}) async-start(bf16[64,2,2,32,128]{4,3,2,1,0:T(8,128)(2,1)} %bitcast.69), calls=%async_computation.2 | async-start | bytes 4194304 | tf_op jit(solution)/shard_map/all_to_all | solution.py:355
  63.7 2.3 gather_fusion
  66.0 4.0 %fusion.55 = (bf16[768,512]{0,1:T(8,128)(2,1)S(1)}, f32[768,512]{0,1:T(8,128)}) fusion(bf16[768,1024]{1,0:T(8,128)(2,1)} %bitcast.75, bf16[2,1024,1,512]{3,1,2,0:T(8,128)(2,1)} %param.7), kind=kOutput, calls=%fused_computation.100 | convolution fusion | flops 807272448 | bytes 4980736 | tf_op jit(solution)/shard_map/dot_general | solution.py:364
  70.1 0.9 copy-done.1
  71.0 39.0 %all-to-all-done.2 = bf16[64,2,2,32,128]{4,3,2,1,0:T(8,128)(2,1)} async-done(((bf16[64,2,2,32,128]{4,3,2,1,0:T(8,128)(2,1)}), bf16[64,2,2,32,128]{4,3,2,1,0:T(8,128)(2,1)}, u32[]{:S(2)}, u32[]{:S(2)}) %all-to-all-start.2) | async-done | bytes 2097184 | tf_op jit(solution)/shard_map/all_to_all | solution.py:355
  110.0 11.0 %all-to-all-start.1 = ((bf16[64,2,2,32,128]{4,3,2,1,0:T(8,128)(2,1)}), bf16[64,2,2,32,128]{4,3,2,1,0:T(8,128)(2,1)}, u32[]{:S(2)}, u32[]{:S(2)}) async-start(bf16[64,2,2,32,128]{4,3,2,1,0:T(8,128)(2,1)} %bitcast.68), calls=%async_computation.1 | async-start | bytes 4194304 | tf_op jit(solution)/shard_map/all_to_all | solution.py:355
  121.5 2.3 gather_fusion.2
  123.9 1.1 fusion.54
  125.0 2.6 %fusion.17 = f32[16,48,128]{2,1,0:T(8,128)} fusion(bf16[16,128,128]{2,1,0:T(8,128)(2,1)} %bitcast.81, bf16[16,48,128]{2,1,0:T(8,128)(2,1)S(1)} %bitcast.85, bf16[16,128,128]{2,1,0:T(8,128)(2,1)} %bitcast.80, f32[16]{0:T(128)S(1)} %add_convert_fusion, pred[16,128]{1,0:T(8,128)(4,1)S(1)} %iota_compare_fusion.2), kind=kOutput, calls=%fused_computation.35 | convolution fusion | flops 51118080 | bytes 1640512 | tf_op jit(solution)/shard_map/rqt,rtd->rqd/dot_general | solution.py:384
  127.6 1.2 copy.40
  129.1 0.7 copy-done.5
  129.8 2.8 %convolution_convert_fusion.1 = bf16[768,1024]{1,0:T(8,128)(2,1)} fusion(bf16[2,1,128,1024]{3,2,1,0:T(8,128)(2,1)S(1)} %copy-done.5, f32[768,512]{0,1:T(8,128)} %get-tuple-element.34, f32[768]{0:T(1024)S(1)} %add_rsqrt_fusion.1, f32[768]{0:T(1024)S(1)} %broadcast_multiply_fusion.1, f32[768,128]{0,1:T(8,128)S(1)} %copy.40, ...), kind=kOutput, calls=%fused_computation.5 | convolution fusion | flops 202801152 | bytes 2830336 | tf_op jit(solution)/shard_map/dot_general | solution.py:396
  132.6 67.0 %shard_map.65 = (bf16[2,48,1024]{2,1,0:T(8,128)(2,1)}, bf16[8,2,48,1024]{3,2,1,0:T(8,128)(2,1)}) custom-call(bf16[8,2,48,1024]{3,2,1,0:T(8,128)(2,1)} %bitcast.70, bf16[2,48,1024]{2,1,0:T(8,128)(2,1)} %bitcast.74), custom_call_target="tpu_custom_call" | custom-call | tf_op jit(solution)/shard_map/pallas_call | solution.py:307
  199.6 4.1 %fusion.56 = (bf16[768,512]{0,1:T(8,128)(2,1)S(1)}, f32[768,512]{0,1:T(8,128)}) fusion(bf16[768,1024]{1,0:T(8,128)(2,1)} %bitcast.86, bf16[2,1024,1,512]{3,1,2,0:T(8,128)(2,1)} %param.7), kind=kOutput, calls=%fused_computation.101 | convolution fusion | flops 807272448 | bytes 4980736 | tf_op jit(solution)/shard_map/dot_general | solution.py:364
  203.9 0.6 copy-done.3
  204.6 2.3 gather_fusion.3
  206.9 1.1 fusion.53
  208.0 2.6 %fusion.16 = f32[16,48,128]{2,1,0:T(8,128)} fusion(bf16[16,128,128]{2,1,0:T(8,128)(2,1)} %bitcast.79, bf16[16,48,128]{2,1,0:T(8,128)(2,1)S(1)} %bitcast.84, bf16[16,128,128]{2,1,0:T(8,128)(2,1)} %bitcast.78, f32[16]{0:T(128)S(1)} %add_convert_fusion, pred[16,128]{1,0:T(8,128)(4,1)S(1)} %iota_compare_fusion.2), kind=kOutput, calls=%fused_computation.30 | convolution fusion | flops 51118080 | bytes 1640512 | tf_op jit(solution)/shard_map/rqt,rtd->rqd/dot_general | solution.py:384
  210.7 1.2 copy.44
  212.1 2.8 %convolution_convert_fusion = bf16[768,1024]{1,0:T(8,128)(2,1)} fusion(bf16[2,1,128,1024]{3,2,1,0:T(8,128)(2,1)} %param.8, f32[768,512]{0,1:T(8,128)} %get-tuple-element.36, f32[768]{0:T(1024)S(1)} %add_rsqrt_fusion, f32[768]{0:T(1024)S(1)} %broadcast_multiply_fusion, f32[768,128]{0,1:T(8,128)S(1)} %copy.44, bf16[768,512]{0,1:T(8,128)(2,1)S(1)} %copy-done.4, ...), kind=kOutput, calls=%fused_computation.4 | convolution fusion | flops 202801152 | bytes 2830336 | tf_op jit(solution)/shard_map/dot_general | solution.py:396
  214.9 27.9 %shard_map.66 = bf16[2,48,1024]{2,1,0:T(8,128)(2,1)} custom-call(bf16[8,2,48,1024]{3,2,1,0:T(8,128)(2,1)} %bitcast.71, bf16[2,48,1024]{2,1,0:T(8,128)(2,1)} %get-tuple-element.24.hidden), custom_call_target="tpu_custom_call" | custom-call | tf_op jit(solution)/shard_map/pallas_call | solution.py:307
  242.8 1.6 copy.50
  (45 shorter events, 1.8 us)
Async XLA Ops:
  0.0 51.7 %copy-start = (bf16[2,64,1,2,32,128]{5,4,3,2,1,0:T(8,128)(2,1)S(1)}, bf16[2,64,1,2,32,128]{5,4,3,2,1,0:T(8,128)(2,1)}, u32[]{:S(2)}) copy-start(bf16[2,64,1,2,32,128]{5,4,3,2,1,0:T(8,128)(2,1)} %param.9) | copy-start | bytes 6291460
  2.1 48.2 %all-to-all-start = ((s32[64,1,2]{2,1,0:T(1,128)}), s32[64,1,2]{2,1,0:T(1,128)S(1)}, u32[]{:S(2)}, u32[]{:S(2)}) async-start(s32[64,1,2]{2,1,0:T(1,128)} %bitcast), calls=%async_computation | async-start | bytes 65536 | tf_op jit(solution)/shard_map/all_to_all | solution.py:347
  53.9 56.1 %all-to-all-start.2 = ((bf16[64,2,2,32,128]{4,3,2,1,0:T(8,128)(2,1)}), bf16[64,2,2,32,128]{4,3,2,1,0:T(8,128)(2,1)}, u32[]{:S(2)}, u32[]{:S(2)}) async-start(bf16[64,2,2,32,128]{4,3,2,1,0:T(8,128)(2,1)} %bitcast.69), calls=%async_computation.2 | async-start | bytes 4194304 | tf_op jit(solution)/shard_map/all_to_all | solution.py:355
  70.1 0.9 copy-start.1
  110.0 11.1 %copy-start.6 = (s32[16]{0:T(128)S(1)}, s32[16]{0:T(128)}, u32[]{:S(2)}) copy-start(s32[16]{0:T(128)} %param.11) | copy-start | bytes 196
  110.0 93.7 %all-to-all-start.1 = ((bf16[64,2,2,32,128]{4,3,2,1,0:T(8,128)(2,1)}), bf16[64,2,2,32,128]{4,3,2,1,0:T(8,128)(2,1)}, u32[]{:S(2)}, u32[]{:S(2)}) async-start(bf16[64,2,2,32,128]{4,3,2,1,0:T(8,128)(2,1)} %bitcast.68), calls=%async_computation.1 | async-start | bytes 4194304 | tf_op jit(solution)/shard_map/all_to_all | solution.py:355
  125.0 3.8 %copy-start.2 = (bf16[768,512]{0,1:T(8,128)(2,1)S(1)}, bf16[768,512]{0,1:T(8,128)(2,1)}, u32[]{:S(2)}) copy-start(bf16[768,512]{0,1:T(8,128)(2,1)} %copy-done.1) | copy-start | bytes 2359300
  128.8 1.0 copy-start.5
  203.7 0.9 copy-start.3
  208.0 3.8 %copy-start.4 = (bf16[768,512]{0,1:T(8,128)(2,1)S(1)}, bf16[768,512]{0,1:T(8,128)(2,1)}, u32[]{:S(2)}) copy-start(bf16[768,512]{0,1:T(8,128)(2,1)} %copy-done.3) | copy-start | bytes 2359300

commit v5 on v4

--- a/solution.py
+++ b/solution.py
@@ -204,8 +204,10 @@
     return sums
 
 
-def gather_kernel(own, out, *scratch):
+def gather_kernel(hidden, out, own, *scratch):
     near = neighbours()
+    for half in range(2):
+        own[half] = layer_norm(wide(hidden[half])).astype(jnp.bfloat16)
     greet(near)
     gather_phase(near, own, out, *scratch)
 
@@ -294,8 +296,8 @@
     one = jax.ShapeDtypeStruct((2,) + halves, jnp.bfloat16)
     whole = jax.ShapeDtypeStruct((group, 2) + halves, jnp.bfloat16)
     if terms is None:
-        kernel, shapes, scratch = gather_kernel, [whole], gathering
-        given = [layer_norm(hidden.astype(jnp.float32)).astype(jnp.bfloat16).reshape(one.shape)]
+        kernel, shapes, scratch = gather_kernel, [whole], [block] + gathering
+        given = [hidden.reshape(one.shape)]
     else:
         given = [terms.reshape(whole.shape), hidden.reshape(one.shape)]
         if gather:

time: 245 us -> 242 us (0.988)
  other arithmetic: 5.62 us -> 1.64 us
  transfers between devices with their start and end apart: 3 -> 3, of which waited for: 1 -> 1; matrix products, arithmetic and copies ran while one was open for 10% -> 9% of each run, Pallas kernels for 40% -> 41%
where the time goes in v5:
time: 242 us; the launch traced here: 241 us
  Pallas kernels  127 us (52%)
  waiting for transfers between devices  39 us (16%)
  starting transfers between devices  33.2 us (14%)
  local copies, waits for them, and re-layouts  20.7 us (9%)
  matrix products  19 us (8%)
    pallas_call x3, Pallas kernels, exchange(): pl.pallas_call(kernel, out_shape=shapes, in_specs=[in_vmem] * len(given),...  127 us
    all_to_all x2, waiting for transfers between devices, history_of(): lax.all_to_all(rows, 'pages', split_axis=0, concat_axis=0, tiled=True)  39 us
    all_to_all x2, starting transfers between devices, history_of(): lax.all_to_all(rows, 'pages', split_axis=0, concat_axis=0, tiled=True)  20.8 us
    all_to_all x1, starting transfers between devices, on_device(): lax.all_to_all(asked.reshape(readers, capacity), 'pages', split_axis=0, c...  12.4 us
    dot_general x2, matrix products, on_device(): jnp.dot(ready, weights_in, preferred_element_type=jnp.float32)  8.08 us
    dot_general x2, matrix products, on_device(): terms = jnp.dot(gated_rows, weights_out, preferred_element_type=jnp.float32)  5.64 us
    dot_general x2, matrix products, on_device(): jnp.einsum('rqt,rtd->rqd', weights, hist_values, preferred_element_type=j...  5.27 us
    unnamed x16, local copies, waits for them, and re-layouts  4.84 us
  transfers between devices with their start and end apart: 3, of which 1 were waited for; matrix products, arithmetic and copies ran while one was open for 9% of the time, Pallas kernels for 41%

profile of v5, /device:TPU:96, one launch (start us, length us, event | category | flops | bytes accessed | tf_op | source)
XLA Modules:
  0.0 240.7 jit_solution(12574694570397057369)
XLA Ops:
  0.0 0.9 copy.34
  1.0 0.2 convert_reduce_fusion
  1.3 0.8 all_to_all.12
  2.1 12.4 %all-to-all-start = ((s32[64,1,2]{2,1,0:T(1,128)}), s32[64,1,2]{2,1,0:T(1,128)S(1)}, u32[]{:S(2)}, u32[]{:S(2)}) async-start(s32[64,1,2]{2,1,0:T(1,128)} %bitcast), calls=%async_computation | async-start | bytes 65536 | tf_op jit(solution)/shard_map/all_to_all | solution.py:349
  14.5 32.0 %shard_map.64 = bf16[8,2,48,1024]{3,2,1,0:T(8,128)(2,1)} custom-call(bf16[2,48,1024]{2,1,0:T(8,128)(2,1)} %bitcast.74), custom_call_target="tpu_custom_call" | custom-call | tf_op jit(solution)/shard_map/pallas_call | solution.py:309
  46.5 0.5 broadcast.429
  47.0 0.7 reduce.3
  47.9 2.2 gather_fusion.1
  50.2 9.8 %all-to-all-start.2 = ((bf16[64,2,2,32,128]{4,3,2,1,0:T(8,128)(2,1)}), bf16[64,2,2,32,128]{4,3,2,1,0:T(8,128)(2,1)}, u32[]{:S(2)}, u32[]{:S(2)}) async-start(bf16[64,2,2,32,128]{4,3,2,1,0:T(8,128)(2,1)} %bitcast.68), calls=%async_computation.2 | async-start | bytes 4194304 | tf_op jit(solution)/shard_map/all_to_all | solution.py:357
  60.0 2.3 gather_fusion
  62.3 4.0 %fusion.51 = (bf16[768,512]{0,1:T(8,128)(2,1)S(1)}, f32[768,512]{0,1:T(8,128)}) fusion(bf16[768,1024]{1,0:T(8,128)(2,1)} %bitcast.73, bf16[2,1024,1,512]{3,1,2,0:T(8,128)(2,1)} %param.7), kind=kOutput, calls=%fused_computation.92 | convolution fusion | flops 807272448 | bytes 4980736 | tf_op jit(solution)/shard_map/dot_general | solution.py:366
  66.3 0.9 copy-done.1
  67.3 39.0 %all-to-all-done.2 = bf16[64,2,2,32,128]{4,3,2,1,0:T(8,128)(2,1)} async-done(((bf16[64,2,2,32,128]{4,3,2,1,0:T(8,128)(2,1)}), bf16[64,2,2,32,128]{4,3,2,1,0:T(8,128)(2,1)}, u32[]{:S(2)}, u32[]{:S(2)}) %all-to-all-start.2) | async-done | bytes 2097184 | tf_op jit(solution)/shard_map/all_to_all | solution.py:357
  106.3 11.0 %all-to-all-start.1 = ((bf16[64,2,2,32,128]{4,3,2,1,0:T(8,128)(2,1)}), bf16[64,2,2,32,128]{4,3,2,1,0:T(8,128)(2,1)}, u32[]{:S(2)}, u32[]{:S(2)}) async-start(bf16[64,2,2,32,128]{4,3,2,1,0:T(8,128)(2,1)} %bitcast.67), calls=%async_computation.1 | async-start | bytes 4194304 | tf_op jit(solution)/shard_map/all_to_all | solution.py:357
  117.6 0.2 copy.36
  117.8 2.3 gather_fusion.2
  120.1 1.1 fusion.50
  121.2 2.6 %fusion.13 = f32[16,48,128]{2,1,0:T(8,128)} fusion(bf16[16,128,128]{2,1,0:T(8,128)(2,1)} %bitcast.80, bf16[16,48,128]{2,1,0:T(8,128)(2,1)S(1)} %bitcast.84, bf16[16,128,128]{2,1,0:T(8,128)(2,1)} %bitcast.79, f32[16]{0:T(128)S(1)} %add_convert_fusion, pred[16,128]{1,0:T(8,128)(4,1)S(1)} %iota_compare_fusion.2), kind=kOutput, calls=%fused_computation.29 | convolution fusion | flops 51118080 | bytes 1640512 | tf_op jit(solution)/shard_map/rqt,rtd->rqd/dot_general | solution.py:386
  123.9 1.2 copy.40
  125.3 0.7 copy-done.5
  126.1 2.8 %convolution_convert_fusion.1 = bf16[768,1024]{1,0:T(8,128)(2,1)} fusion(bf16[2,1,128,1024]{3,2,1,0:T(8,128)(2,1)S(1)} %copy-done.5, f32[768,512]{0,1:T(8,128)} %get-tuple-element.34, f32[768]{0:T(1024)S(1)} %add_rsqrt_fusion.1, f32[768]{0:T(1024)S(1)} %broadcast_multiply_fusion.1, f32[768,128]{0,1:T(8,128)S(1)} %copy.40, ...), kind=kOutput, calls=%fused_computation.5 | convolution fusion | flops 202801152 | bytes 2830336 | tf_op jit(solution)/shard_map/dot_general | solution.py:398
  128.9 67.0 %shard_map.65 = (bf16[2,48,1024]{2,1,0:T(8,128)(2,1)}, bf16[8,2,48,1024]{3,2,1,0:T(8,128)(2,1)}) custom-call(bf16[8,2,48,1024]{3,2,1,0:T(8,128)(2,1)} %bitcast.69, bf16[2,48,1024]{2,1,0:T(8,128)(2,1)} %bitcast.75), custom_call_target="tpu_custom_call" | custom-call | tf_op jit(solution)/shard_map/pallas_call | solution.py:309
  195.9 4.1 %fusion.52 = (bf16[768,512]{0,1:T(8,128)(2,1)S(1)}, f32[768,512]{0,1:T(8,128)}) fusion(bf16[768,1024]{1,0:T(8,128)(2,1)} %bitcast.85, bf16[2,1024,1,512]{3,1,2,0:T(8,128)(2,1)} %param.7), kind=kOutput, calls=%fused_computation.93 | convolution fusion | flops 807272448 | bytes 4980736 | tf_op jit(solution)/shard_map/dot_general | solution.py:366
  200.0 0.2 copy.41
  200.2 0.6 copy-done.3
  200.8 2.3 gather_fusion.3
  203.2 1.1 fusion.49
  204.3 2.6 %fusion.12 = f32[16,48,128]{2,1,0:T(8,128)} fusion(bf16[16,128,128]{2,1,0:T(8,128)(2,1)} %bitcast.78, bf16[16,48,128]{2,1,0:T(8,128)(2,1)S(1)} %bitcast.83, bf16[16,128,128]{2,1,0:T(8,128)(2,1)} %bitcast.77, f32[16]{0:T(128)S(1)} %add_convert_fusion, pred[16,128]{1,0:T(8,128)(4,1)S(1)} %iota_compare_fusion.2), kind=kOutput, calls=%fused_computation.24 | convolution fusion | flops 51118080 | bytes 1640512 | tf_op jit(solution)/shard_map/rqt,rtd->rqd/dot_general | solution.py:386
  206.9 1.2 copy.44
  208.3 2.8 %convolution_convert_fusion = bf16[768,1024]{1,0:T(8,128)(2,1)} fusion(bf16[2,1,128,1024]{3,2,1,0:T(8,128)(2,1)} %param.8, f32[768,512]{0,1:T(8,128)} %get-tuple-element.36, f32[768]{0:T(1024)S(1)} %add_rsqrt_fusion, f32[768]{0:T(1024)S(1)} %broadcast_multiply_fusion, f32[768,128]{0,1:T(8,128)S(1)} %copy.44, bf16[768,512]{0,1:T(8,128)(2,1)S(1)} %copy-done.4, ...), kind=kOutput, calls=%fused_computation.4 | convolution fusion | flops 202801152 | bytes 2830336 | tf_op jit(solution)/shard_map/dot_general | solution.py:398
  211.2 27.9 %shard_map.66 = bf16[2,48,1024]{2,1,0:T(8,128)(2,1)} custom-call(bf16[8,2,48,1024]{3,2,1,0:T(8,128)(2,1)} %bitcast.70, bf16[2,48,1024]{2,1,0:T(8,128)(2,1)} %get-tuple-element.24.hidden), custom_call_target="tpu_custom_call" | custom-call | tf_op jit(solution)/shard_map/pallas_call | solution.py:309
  239.1 1.6 copy.50
  (40 shorter events, 1.2 us)
Async XLA Ops:
  0.0 47.9 %copy-start = (bf16[2,64,1,2,32,128]{5,4,3,2,1,0:T(8,128)(2,1)S(1)}, bf16[2,64,1,2,32,128]{5,4,3,2,1,0:T(8,128)(2,1)}, u32[]{:S(2)}) copy-start(bf16[2,64,1,2,32,128]{5,4,3,2,1,0:T(8,128)(2,1)} %param.9) | copy-start | bytes 6291460
  2.1 44.4 %all-to-all-start = ((s32[64,1,2]{2,1,0:T(1,128)}), s32[64,1,2]{2,1,0:T(1,128)S(1)}, u32[]{:S(2)}, u32[]{:S(2)}) async-start(s32[64,1,2]{2,1,0:T(1,128)} %bitcast), calls=%async_computation | async-start | bytes 65536 | tf_op jit(solution)/shard_map/all_to_all | solution.py:349
  50.2 56.1 %all-to-all-start.2 = ((bf16[64,2,2,32,128]{4,3,2,1,0:T(8,128)(2,1)}), bf16[64,2,2,32,128]{4,3,2,1,0:T(8,128)(2,1)}, u32[]{:S(2)}, u32[]{:S(2)}) async-start(bf16[64,2,2,32,128]{4,3,2,1,0:T(8,128)(2,1)} %bitcast.68), calls=%async_computation.2 | async-start | bytes 4194304 | tf_op jit(solution)/shard_map/all_to_all | solution.py:357
  66.3 0.9 copy-start.1
  106.2 11.1 %copy-start.6 = (s32[16]{0:T(128)S(1)}, s32[16]{0:T(128)}, u32[]{:S(2)}) copy-start(s32[16]{0:T(128)} %param.11) | copy-start | bytes 196
  106.3 93.7 %all-to-all-start.1 = ((bf16[64,2,2,32,128]{4,3,2,1,0:T(8,128)(2,1)}), bf16[64,2,2,32,128]{4,3,2,1,0:T(8,128)(2,1)}, u32[]{:S(2)}, u32[]{:S(2)}) async-start(bf16[64,2,2,32,128]{4,3,2,1,0:T(8,128)(2,1)} %bitcast.67), calls=%async_computation.1 | async-start | bytes 4194304 | tf_op jit(solution)/shard_map/all_to_all | solution.py:357
  121.2 3.8 %copy-start.2 = (bf16[768,512]{0,1:T(8,128)(2,1)S(1)}, bf16[768,512]{0,1:T(8,128)(2,1)}, u32[]{:S(2)}) copy-start(bf16[768,512]{0,1:T(8,128)(2,1)} %copy-done.1) | copy-start | bytes 2359300
  125.0 1.0 copy-start.5
  199.9 0.9 copy-start.3
  204.3 3.8 %copy-start.4 = (bf16[768,512]{0,1:T(8,128)(2,1)S(1)}, bf16[768,512]{0,1:T(8,128)(2,1)}, u32[]{:S(2)}) copy-start(bf16[768,512]{0,1:T(8,128)(2,1)} %copy-done.3) | copy-start | bytes 2359300
